TPU v7x, 32 devices: a whole 2x2x4 slice. The times are simulated.
32 devices in a mesh: patch: 8 (over z, x), lev: 4 (over y, core).
Axes of the slice: x: 2, y: 2, z: 4, core: 2. Of those that a mesh axis runs over, the one named last changes fastest.
Arguments:
- tracer_field: float32 [80, 3, 16384], P('lev', None, 'patch'), may hold values from -6 to 6
- send_coarse1: int32 [8, 2, 128], P('patch'), may hold values from 0 to 1023
- send_detail1: int32 [8, 2, 128], P('patch'), may hold values from 0 to 1023
- send_coarse2: int32 [8, 2, 64], P('patch'), may hold values from 0 to 511
- send_detail2: int32 [8, 2, 64], P('patch'), may hold values from 0 to 511
- predict_links1: int32 [8, 8192], P(None, 'patch'), may hold values from 0 to 1279
- predict_weights1: float32 [8, 8192], P(None, 'patch'), may hold values from 0.02 to 0.22
- update_links1: int32 [8, 8192], P(None, 'patch'), may hold values from 0 to 1279
- update_weights1: float32 [8, 8192], P(None, 'patch'), may hold values from 0.02 to 0.14
- predict_links2: int32 [8, 4096], P(None, 'patch'), may hold values from 0 to 639
- predict_weights2: float32 [8, 4096], P(None, 'patch'), may hold values from 0.02 to 0.22
- update_links2: int32 [8, 4096], P(None, 'patch'), may hold values from 0 to 639
- update_weights2: float32 [8, 4096], P(None, 'patch'), may hold values from 0.02 to 0.14
Outputs:
- coefficients: float32 [80, 3, 16384], P(None, None, ('patch', 'lev'))
Inputs may be any that keep to these rules, and one draw needn't show every extreme that they name: `send_coarse1`: row lists index a patch's own coarse or detail rows of that level. `predict_links1`: links index the patch's own rows first, then the 128 rows from the left neighbour, then the 128 from the right. `predict_links2`: links index the patch's own rows first, then the 64 rows from the left neighbour, then the 64 from the right.
All inputs are finite; a program needn't handle non-finite values.
Results may differ from a plain program's by a relative error of at most 0.00007.
Values sent between devices are 32-bit elements; how exact they have to be, the bound alone decides.
A program may use at most 64 MiB of HBM per device.

v0:
```python
import functools

import jax
import jax.numpy as jnp
import ml_dtypes
import numpy as np
from jax import lax
from jax.experimental import pallas as pl
from jax.experimental.pallas import tpu as pltpu
from jax.sharding import PartitionSpec as P

LANES = 128
SUB = 8
MESH = pl.DeviceIdType.MESH


def cosine_table(length):
    rows = np.arange(length, dtype=np.float64)[:, None]
    columns = np.arange(length, dtype=np.float64)[None, :]
    matrix = np.cos(np.pi * (columns + 0.5) * rows / length) * np.sqrt(2.0 / length)
    matrix[0] *= np.sqrt(0.5)
    return matrix


def spread_table(levels, tracers, groups, padded):
    own = levels // groups
    table = cosine_table(levels).reshape(levels, groups, own)
    wide = np.zeros((tracers, levels, groups, padded))
    for t in range(tracers):
        wide[t, :, :, t * own : (t + 1) * own] = table
    wide = wide.reshape(levels * tracers, groups * padded).astype(np.float32)
    high = wide.astype(ml_dtypes.bfloat16)
    low = (wide - high.astype(np.float32)).astype(ml_dtypes.bfloat16)
    return high, low


def halves(x):
    high = x.astype(jnp.bfloat16)
    low = (x - high.astype(jnp.float32)).astype(jnp.bfloat16)
    return high, low


def build(links, weights, merged, w_high, w_low, first, count, blocks, base=0, shift=0):
    slots = links.shape[0]
    groups = -(-blocks // SUB)

    def column(tile, _):
        cols = pl.ds(pl.multiple_of(first + tile * LANES, LANES), LANES)
        into = pl.ds(pl.multiple_of(first + shift + tile * LANES, LANES), LANES)
        lane = []
        block = []
        weight = []
        for k in range(slots):
            link = jnp.broadcast_to(links[k : k + 1, cols], (SUB, LANES))
            lane.append(link & (LANES - 1))
            block.append((link >> 7) - base)
            weight.append(jnp.broadcast_to(weights[k : k + 1, cols], (SUB, LANES)))
        which = lax.broadcasted_iota(jnp.int32, (SUB, LANES), 0)
        for g in range(groups):
            placed = []
            for k in range(slots):
                mine = jnp.where(block[k] == which + g * SUB, weight[k], 0.0)
                total = mine
                for j in range(k):
                    total = total + jnp.where(lane[j] == lane[k], placed[j], 0.0)
                placed.append(mine)
                merged[k, g * SUB : (g + 1) * SUB, :] = total
        lane2 = [jnp.concatenate([v, v], axis=0) for v in lane]

        def strip(s, _):
            rows16 = lax.broadcasted_iota(jnp.int32, (2 * SUB, LANES), 0) + s * (2 * SUB)
            masks = [lane2[k] == rows16 for k in range(slots)]
            for b in range(blocks):
                total = jnp.zeros((2 * SUB, LANES), jnp.float32)
                for k in range(slots):
                    row = jnp.broadcast_to(merged[k, b : b + 1, :], (2 * SUB, LANES))
                    total = jnp.where(masks[k], row, total)
                high, low = halves(total)
                place = pl.ds(pl.multiple_of(b * LANES + s * (2 * SUB), 2 * SUB), 2 * SUB)
                w_high[place, into] = high
                w_low[place, into] = low
            return 0

        lax.fori_loop(0, LANES // (2 * SUB), strip, 0)
        return 0

    lax.fori_loop(0, count // LANES, column, 0)


def picked(source, start, blocks, index, out):
    lane = jnp.broadcast_to(index & (LANES - 1), (SUB, LANES))
    block = jnp.broadcast_to(index >> 7, (SUB, LANES))
    for r in range(source.shape[0] // SUB):
        rows = slice(r * SUB, (r + 1) * SUB)
        got = None
        for b in range(blocks):
            cols = slice(start + b * LANES, start + (b + 1) * LANES)
            t = jnp.take_along_axis(source[rows, cols], lane, axis=1)
            got = t if got is None else jnp.where(block == b, t, got)
        out[rows, :] = got


def put(ext, padded, at, value):
    high, low = halves(value)
    width = value.shape[1]
    ext[0:padded, at : at + width] = high
    ext[padded : 2 * padded, at : at + width] = low


def product(ext, padded, span, w_high, w_low, cols):
    k = slice(*span)
    both = jnp.dot(ext[:, k], w_high[k, cols], preferred_element_type=jnp.float32)
    rest = jnp.dot(ext[0:padded, k], w_low[k, cols], preferred_element_type=jnp.float32)
    return both[0:padded] + both[padded : 2 * padded] + rest


def small(value, m_high, m_low):
    padded = value.shape[0]
    high, low = halves(value)
    both = jnp.concatenate([high, low], axis=0)
    both = jnp.dot(both, m_high, preferred_element_type=jnp.float32)
    rest = jnp.dot(high, m_low, preferred_element_type=jnp.float32)
    return both[0:padded] + both[padded : 2 * padded] + rest


def body(
    n_patch, n_lev, levels,
    field, sc1, sd1, sc2, sd2, pl1, pw1, ul1, uw1, pl2, pw2, ul2, uw2,
    gathered,
    xs, ext, merged, p1h, p1l, u1h, u1l, p2h, p2l, u2h, u2l,
    det1, sm1, det2, sm2, hsend, hrecv,
    ext2, glink, gweight, rlink, rweight, mh, ml, part, full1, full2, done,
    ms_sem, mr_sem,
    hs_sem, hr_sem, as_sem, ar_sem,
):
    tracers, own, cells = field.shape
    rows = own * tracers
    padded = xs.shape[0]
    n1 = cells // 2
    n2 = cells // 4
    halo1 = sc1.shape[2]
    halo2 = sc2.shape[2]
    chunk = cells // n_lev
    me = lax.axis_index("lev")
    patch = lax.axis_index("patch")
    left = lax.rem(patch + n_patch - 1, n_patch)
    right = lax.rem(patch + 1, n_patch)

    barrier = pltpu.get_barrier_semaphore()
    for neighbour in (left, right):
        pl.semaphore_signal(barrier, inc=1, device_id={"patch": neighbour}, device_id_type=MESH)
    for d in range(1, n_lev):
        pl.semaphore_signal(
            barrier, inc=1, device_id={"lev": lax.rem(me + d, n_lev)}, device_id_type=MESH
        )

    if padded > rows:
        edge = rows // SUB * SUB
        xs[edge:padded, :] = jnp.zeros((padded - edge, cells), jnp.float32)
    for t in range(tracers):
        xs[t * own : (t + 1) * own, :] = field[t]

    def copy_to(phase, side):
        return pltpu.make_async_remote_copy(
            src_ref=hsend.at[phase, side],
            dst_ref=hrecv.at[phase, side],
            send_sem=hs_sem.at[phase, side],
            recv_sem=hr_sem.at[phase, side],
            device_id={"patch": left if side else right},
            device_id_type=MESH,
        )

    def meta_to(side):
        return [
            pltpu.make_async_remote_copy(
                src_ref=mine.at[side],
                dst_ref=theirs.at[side],
                send_sem=ms_sem.at[which, side],
                recv_sem=mr_sem.at[which, side],
                device_id={"patch": left if side else right},
                device_id_type=MESH,
            )
            for which, (mine, theirs) in enumerate(((glink, rlink), (gweight, rweight)))
        ]

    def both_sides(step):
        @pl.when(patch == 0)
        def _():
            step(1)
            step(0)

        @pl.when(patch != 0)
        def _():
            step(0)
            step(1)

    outgoing = []

    def scatter(source, base):
        for piece in range(source.shape[1] // chunk):
            d = base // chunk + piece
            part = source.at[:, piece * chunk : (piece + 1) * chunk]
            copy = pltpu.make_async_remote_copy(
                src_ref=part,
                dst_ref=gathered.at[me],
                send_sem=as_sem.at[d],
                recv_sem=ar_sem.at[me],
                device_id={"lev": d},
                device_id_type=MESH,
            )
            outgoing.append((d, copy))

            @pl.when(me != d)
            def _():
                copy.start()

            @pl.when(me == d)
            def _():
                gathered[d] = part[...]

    b1 = n1 // LANES
    b2 = n2 // LANES
    e1 = n1 + 2 * halo1
    e2 = n2 + 2 * halo2
    wide = 256

    def predict(into, start, values, depth, w_high, w_low, n, add):
        for c in range(0, n, wide):
            cols = slice(start + c, start + c + wide)
            source = ext if n1 <= w_high.shape[1] else ext2
            got = product(source, padded, depth, w_high, w_low, cols)
            old = values(cols)
            into[:, cols] = old + got if add else old - got

    def fine1(cols):
        return xs[:, cols]

    def coarse1(cols):
        return xs[:, n1 + cols.start : n1 + cols.stop]

    def fine2(cols):
        return sm1[:, cols]

    def coarse2(cols):
        return sm1[:, n2 + cols.start : n2 + cols.stop]

    def held(ref):
        return lambda cols: ref[:, cols]

    h1 = 2 * halo1 // LANES
    h2 = 2 * halo2 // LANES
    lower = lax.broadcasted_iota(jnp.int32, (padded, LANES), 1) < halo2

    def tail(phase, side):
        if phase == 2:
            return slice(0, LANES)
        return slice(side * LANES, (side + 1) * LANES)

    def sided(phase, side, value):
        if phase != 2:
            return value
        return jnp.where(lower, value, 0.0) if side == 0 else jnp.where(lower, 0.0, value)

    def halo_part(phase, side, column, value):
        cols = slice(column * LANES, (column + 1) * LANES)
        k = tail(phase, side)
        return small(sided(phase, side, value), mh[phase, k, cols], ml[phase, k, cols])

    def two(send):
        return jnp.concatenate([send[0, 1:2, :], send[0, 0:1, :]], axis=1)

    def share(phase, links, weights, start, blocks, indices):
        for side, index in enumerate(indices):
            picked(links, start, blocks, index, glink.at[side, phase])
            picked(weights, start, blocks, index, gweight.at[side, phase])

    picked(xs, n1, b1, sc1[0, 1:2, :], hsend.at[0, 0])
    picked(xs, n1, b1, sc1[0, 0:1, :], hsend.at[0, 1])
    pl.semaphore_wait(barrier, 2 + n_lev - 1)
    for side in range(2):
        copy_to(0, side).start()
    share(0, pl1, pw1, 0, b1, (sd1[0, 1:2, :], sd1[0, 0:1, :]))
    share(1, ul1, uw1, n2, b2, (two(sc2), two(sc2)))
    share(2, pl2, pw2, 0, b2, (two(sd2), two(sd2)))
    for side in range(2):
        for c in meta_to(side):
            c.start()
    put(ext, padded, 0, xs[:, n1:cells])
    build(pl1, pw1, merged, p1h, p1l, 0, n1, e1 // LANES)
    predict(det1, 0, fine1, (0, n1), p1h, p1l, n1, False)
    picked(det1, 0, b1, sd1[0, 1:2, :], part.at[0])
    picked(det1, 0, b1, sd1[0, 0:1, :], part.at[1])

    def spread(links, weights, phase, column, blocks, base):
        build(
            links, weights, merged, mh.at[phase], ml.at[phase], 0, LANES, blocks, base,
            column * LANES,
        )

    for side in range(2):
        spread(glink.at[side, 0], gweight.at[side, 0], 0, side, h1, b1)

    def step0(side):
        copy_to(0, side).wait_recv()
        hsend[1, side] = part[side] - halo_part(0, side, side, hrecv[0, side])
        copy_to(1, side).start()

    both_sides(step0)
    put(ext, padded, n1, hrecv[0, 0])
    put(ext, padded, n1 + halo1, hrecv[0, 1])
    predict(det1, 0, held(det1), (n1, e1), p1h, p1l, n1, False)
    scatter(det1, 0)

    spread(glink.at[0, 1], gweight.at[0, 1], 1, 0, h1, b1)
    build(ul1, uw1, merged, u1h, u1l, n2, n2, e1 // LANES)
    put(ext, padded, 0, det1[...])
    predict(sm1, n2, coarse1, (0, n1), u1h, u1l, n2, True)
    picked(sm1, n2, b2, two(sc2), part.at[0])
    picked(det1, 0, b1, sd1[0, 1:2, :], full1.at[0])
    picked(det1, 0, b1, sd1[0, 0:1, :], full1.at[1])
    for side in range(2):
        for c in meta_to(side):
            c.wait_recv()
    for side in range(2):
        spread(rlink.at[side, 0], rweight.at[side, 0], 0, 2 + side, h1, b1)
    spread(glink.at[0, 2], gweight.at[0, 2], 2, 0, h2, b2)
    build(pl2, pw2, merged, p2h, p2l, 0, n2, e2 // LANES)
    for side in range(2):
        spread(rlink.at[side, 1], rweight.at[side, 1], 1, 2 + side, h1, b1)

    def step1(side):
        copy_to(1, side).wait_recv()
        value = hrecv[1, side] - halo_part(0, 1 - side, 2 + side, hsend[0, 1 - side])
        done[side] = value
        hsend[2, side] = part[0] + halo_part(1, side, 0, value)
        copy_to(2, side).start()

    both_sides(step1)
    put(ext, padded, n1, done[0])
    put(ext, padded, n1 + halo1, done[1])
    predict(sm1, n2, held(sm1), (n1, e1), u1h, u1l, n2, True)

    build(ul1, uw1, merged, u1h, u1l, 0, n2, e1 // LANES)
    predict(sm1, 0, coarse1, (0, e1), u1h, u1l, n2, True)
    put(ext2, padded, 0, sm1[:, n2:n1])
    picked(sm1, n2, b2, two(sc2), full2)
    predict(det2, 0, fine2, (0, n2), p2h, p2l, n2, False)
    picked(det2, 0, b2, two(sd2), part.at[1])

    def step2(side):
        copy_to(2, side).wait_recv()
        value = hrecv[2, side] + halo_part(1, 1 - side, 2 + side, full1[1 - side])
        done[side] = value
        hsend[3, side] = part[1] - halo_part(2, side, 0, value)
        copy_to(3, side).start()

    both_sides(step2)
    put(ext2, padded, n2, jnp.where(lower, done[0], done[1]))
    predict(det2, 0, held(det2), (n2, e2), p2h, p2l, n2, False)
    scatter(det2, n1)

    put(ext2, padded, 0, det2[...])
    for side in range(2):
        spread(rlink.at[side, 2], rweight.at[side, 2], 2, 2 + side, h2, b2)
    build(ul2, uw2, merged, u2h, u2l, 0, n2, e2 // LANES)
    predict(sm2, 0, coarse2, (0, n2), u2h, u2l, n2, True)

    def step3(side):
        copy_to(3, side).wait_recv()
        done[side] = hrecv[3, side] - halo_part(2, 1 - side, 2 + side, full2[...])

    both_sides(step3)
    put(ext2, padded, n2, jnp.where(lower, done[0], done[1]))
    predict(sm2, 0, held(sm2), (n2, e2), u2h, u2l, n2, True)
    scatter(sm2, n1 + n2)

    for s in range(n_lev):

        @pl.when(me != s)
        def _():
            pltpu.make_async_remote_copy(
                src_ref=gathered.at[s],
                dst_ref=gathered.at[s],
                send_sem=as_sem.at[s],
                recv_sem=ar_sem.at[s],
                device_id={"lev": s},
                device_id_type=MESH,
            ).wait_recv()

    for side in range(2):
        for phase in range(4):
            copy_to(phase, side).wait_send()
        for c in meta_to(side):
            c.wait_send()
    for d, copy in outgoing:

        @pl.when(me != d)
        def _():
            copy.wait_send()


def transform(gathered, t_high, t_low, out):
    groups, padded, chunk = gathered.shape
    tracers, levels, _ = out.shape
    high, low = halves(gathered[...].reshape(groups * padded, chunk))
    for t in range(tracers):
        rows = slice(t * levels, (t + 1) * levels)
        out[t] = (
            jnp.dot(t_high[rows, :], high, preferred_element_type=jnp.float32)
            + jnp.dot(t_high[rows, :], low, preferred_element_type=jnp.float32)
            + jnp.dot(t_low[rows, :], high, preferred_element_type=jnp.float32)
        )


def on_device(n_patch, n_lev, *args):
    field, sc1 = args[0], args[1]
    own, tracers, cells = field.shape
    levels = own * n_lev
    rows = own * tracers
    padded = -(-rows // (2 * SUB)) * (2 * SUB)
    n1, n2 = cells // 2, cells // 4
    e1 = n1 + 2 * sc1.shape[2]
    e2 = n2 + 2 * args[3].shape[2]
    chunk = cells // n_lev
    slots = args[5].shape[0]
    t_high, t_low = spread_table(levels, tracers, n_lev, padded)
    f32, bf16 = jnp.float32, jnp.bfloat16
    gathered = pl.pallas_call(
        functools.partial(body, n_patch, n_lev, levels),
        out_shape=jax.ShapeDtypeStruct((n_lev, padded, chunk), f32),
        in_specs=[pl.BlockSpec(memory_space=pltpu.VMEM)] * 13,
        out_specs=pl.BlockSpec(memory_space=pltpu.VMEM),
        scratch_shapes=[
            pltpu.VMEM((padded, cells), f32),
            pltpu.VMEM((2 * padded, e1), bf16),
            pltpu.VMEM((slots, -(-(e1 // LANES) // SUB) * SUB, LANES), f32),
            pltpu.VMEM((e1, n1), bf16),
            pltpu.VMEM((e1, n1), bf16),
            pltpu.VMEM((e1, n1), bf16),
            pltpu.VMEM((e1, n1), bf16),
            pltpu.VMEM((e2, n2), bf16),
            pltpu.VMEM((e2, n2), bf16),
            pltpu.VMEM((e2, n2), bf16),
            pltpu.VMEM((e2, n2), bf16),
            pltpu.VMEM((padded, n1), f32),
            pltpu.VMEM((padded, n1), f32),
            pltpu.VMEM((padded, n2), f32),
            pltpu.VMEM((padded, n2), f32),
            pltpu.VMEM((4, 2, padded, LANES), f32),
            pltpu.VMEM((4, 2, padded, LANES), f32),
            pltpu.VMEM((2 * padded, e2), bf16),
            pltpu.VMEM((2, 3, slots, LANES), jnp.int32),
            pltpu.VMEM((2, 3, slots, LANES), f32),
            pltpu.VMEM((2, 3, slots, LANES), jnp.int32),
            pltpu.VMEM((2, 3, slots, LANES), f32),
            pltpu.VMEM((3, 2 * LANES, 4 * LANES), bf16),
            pltpu.VMEM((3, 2 * LANES, 4 * LANES), bf16),
            pltpu.VMEM((2, padded, LANES), f32),
            pltpu.VMEM((2, padded, LANES), f32),
            pltpu.VMEM((padded, LANES), f32),
            pltpu.VMEM((2, padded, LANES), f32),
            pltpu.SemaphoreType.DMA((2, 2)),
            pltpu.SemaphoreType.DMA((2, 2)),
            pltpu.SemaphoreType.DMA((4, 2)),
            pltpu.SemaphoreType.DMA((4, 2)),
            pltpu.SemaphoreType.DMA((n_lev,)),
            pltpu.SemaphoreType.DMA((n_lev,)),
        ],
        compiler_params=pltpu.CompilerParams(collective_id=0, has_side_effects=True),
    )(jnp.transpose(field, (1, 0, 2)), *args[1:])
    result = pl.pallas_call(
        transform,
        out_shape=jax.ShapeDtypeStruct((tracers, levels, chunk), f32),
        in_specs=[pl.BlockSpec(memory_space=pltpu.VMEM)] * 3,
        out_specs=pl.BlockSpec(memory_space=pltpu.VMEM),
    )(gathered, jnp.asarray(t_high), jnp.asarray(t_low))
    return jnp.transpose(result, (1, 0, 2))


def solution(mesh):
    in_specs = (P("lev", None, "patch"),)
    in_specs += (P("patch", None, None),) * 4
    in_specs += (P(None, "patch"),) * 8
    out_specs = P(None, None, ("patch", "lev"))
    fn = functools.partial(on_device, mesh.shape["patch"], mesh.shape["lev"])
    return jax.shard_map(
        fn, mesh=mesh, in_specs=in_specs, out_specs=out_specs, check_vma=False
    )
```

profile of v0, /device:TPU:0, one launch (start us, length us, event | category | flops | bytes accessed | tf_op | source)
XLA Modules:
  0.0 30.1 jit_solution(7099970555215190196)
XLA Ops:
  0.0 27.7 %shard_map.145.gathered = f32[4,64,512]{2,1,0:T(8,128)} custom-call(f32[3,20,2048]{2,1,0:T(8,128)} %bitcast.2, s32[1,2,128]{2,1,0:T(2,128)} %sc1.1, s32[1,2,128]{2,1,0:T(2,128)} %sd1.1, s32[1,2,64]{2,1,0:T(2,128)} %sc2.1, s32[1,2,64]{2,1,0:T(2,128)} %sd2.1, s32[8,1024]{1,0:T(8,128)} %pl1.1, f32[8,1024]{1,0:T(8,128)} %pw1.1, s32[8,1024]{1,0:T(8,128)} %ul1.1, ...), custom_call_target="tpu_custom_call" | custom-call | tf_op jit(solution)/shard_map/pallas_call | solution.py:428
  27.7 2.5 %shard_map.146 = f32[3,80,512]{2,1,0:T(8,128)} custom-call(f32[4,64,512]{2,1,0:T(8,128)} %shard_map.145.gathered, bf16[240,256]{1,0:T(8,128)(2,1)} %constant.4.clone.t_high, bf16[240,256]{1,0:T(8,128)(2,1)} %constant.5.clone.t_low), custom_call_target="tpu_custom_call" | custom-call | tf_op jit(solution)/shard_map/pallas_call | solution.py:471
where the time goes:
time: 30.3 us; the launch traced here: 30.1 us
  Pallas kernels  30.1 us (99%)
    pallas_call x1, Pallas kernels, on_device(): pl.pallas_call(functools.partial(body, n_patch, n_lev, levels), out_shape...  27.7 us
    pallas_call x1, Pallas kernels, on_device(): pl.pallas_call(transform, out_shape=jax.ShapeDtypeStruct((tracers, levels...  2.46 us

commit v1 on v0

--- a/solution.py
+++ b/solution.py
@@ -40,51 +40,89 @@
     return high, low
 
 
-def build(links, weights, merged, w_high, w_low, first, count, blocks, base=0, shift=0):
+def along(table, index):
+    numbers = lax.GatherDimensionNumbers(
+        offset_dims=(),
+        collapsed_slice_dims=(0,),
+        start_index_map=(0,),
+        operand_batching_dims=(1,),
+        start_indices_batching_dims=(1,),
+    )
+    mode = lax.GatherScatterMode.PROMISE_IN_BOUNDS
+    return lax.gather(table, index[:, :, None], numbers, (1, 1), mode=mode)
+
+
+def tile(links, weights, merged, cols, blocks):
     slots = links.shape[0]
-    groups = -(-blocks // SUB)
-
-    def column(tile, _):
-        cols = pl.ds(pl.multiple_of(first + tile * LANES, LANES), LANES)
-        into = pl.ds(pl.multiple_of(first + shift + tile * LANES, LANES), LANES)
-        lane = []
-        block = []
-        weight = []
+    lane = []
+    block = []
+    weight = []
+    for k in range(slots):
+        link = jnp.broadcast_to(links[k : k + 1, cols], (SUB, LANES))
+        lane.append(link & (LANES - 1))
+        block.append(link >> 7)
+        weight.append(jnp.broadcast_to(weights[k : k + 1, cols], (SUB, LANES)))
+    which = lax.broadcasted_iota(jnp.int32, (SUB, LANES), 0)
+    same = [[lane[j] == lane[k] for j in range(k)] for k in range(slots)]
+    for g in range(-(-blocks // SUB)):
+        placed = []
         for k in range(slots):
-            link = jnp.broadcast_to(links[k : k + 1, cols], (SUB, LANES))
-            lane.append(link & (LANES - 1))
-            block.append((link >> 7) - base)
-            weight.append(jnp.broadcast_to(weights[k : k + 1, cols], (SUB, LANES)))
-        which = lax.broadcasted_iota(jnp.int32, (SUB, LANES), 0)
-        for g in range(groups):
-            placed = []
-            for k in range(slots):
-                mine = jnp.where(block[k] == which + g * SUB, weight[k], 0.0)
-                total = mine
-                for j in range(k):
-                    total = total + jnp.where(lane[j] == lane[k], placed[j], 0.0)
-                placed.append(mine)
-                merged[k, g * SUB : (g + 1) * SUB, :] = total
-        lane2 = [jnp.concatenate([v, v], axis=0) for v in lane]
-
-        def strip(s, _):
-            rows16 = lax.broadcasted_iota(jnp.int32, (2 * SUB, LANES), 0) + s * (2 * SUB)
-            masks = [lane2[k] == rows16 for k in range(slots)]
-            for b in range(blocks):
-                total = jnp.zeros((2 * SUB, LANES), jnp.float32)
-                for k in range(slots):
-                    row = jnp.broadcast_to(merged[k, b : b + 1, :], (2 * SUB, LANES))
-                    total = jnp.where(masks[k], row, total)
-                high, low = halves(total)
-                place = pl.ds(pl.multiple_of(b * LANES + s * (2 * SUB), 2 * SUB), 2 * SUB)
-                w_high[place, into] = high
-                w_low[place, into] = low
-            return 0
-
-        lax.fori_loop(0, LANES // (2 * SUB), strip, 0)
+            mine = jnp.where(block[k] == which + g * SUB, weight[k], 0.0)
+            total = mine
+            for j in range(k):
+                total = total + jnp.where(same[k][j], placed[j], 0.0)
+            placed.append(mine)
+            merged[k, g * SUB : (g + 1) * SUB, :] = total
+    none = jnp.zeros((2 * SUB - slots, LANES), jnp.float32)
+    tables = [halves(jnp.concatenate([merged[:, b, :], none], axis=0)) for b in range(blocks)]
+    short = [jnp.concatenate([v, v], axis=0).astype(jnp.int16) for v in lane]
+    strips = []
+    for s in range(LANES // (2 * SUB)):
+        rows = lax.broadcasted_iota(jnp.int16, (2 * SUB, LANES), 0) + jnp.int16(s * 2 * SUB)
+        index = jnp.full((2 * SUB, LANES), slots, jnp.int16)
+        for k in range(slots):
+            index = jnp.where(short[k] == rows, jnp.int16(k), index)
+        strips.append(index)
+    return tables, strips
+
+
+def spread(tiles, part, first, last):
+    return jnp.concatenate(
+        [
+            jnp.concatenate(
+                [along(tables[b][part], index) for b in range(first, last) for index in strips],
+                axis=0,
+            )
+            for tables, strips in tiles
+        ],
+        axis=1,
+    )
+
+
+def stage(links, weights, merged, first, count, own, blocks, ext, tail_high, tail_low, emit):
+    padded = ext.shape[0] // 2
+    depth = own * LANES
+
+    def step(t, _):
+        start = pl.multiple_of(first + t * 2 * LANES, 2 * LANES)
+        tiles = [
+            tile(
+                links, weights, merged.at[h],
+                pl.ds(pl.multiple_of(start + h * LANES, LANES), LANES), blocks,
+            )
+            for h in range(2)
+        ]
+        high = spread(tiles, 0, 0, own)
+        low = spread(tiles, 1, 0, own)
+        both = jnp.dot(ext[:, 0:depth], high, preferred_element_type=jnp.float32)
+        rest = jnp.dot(ext[0:padded, 0:depth], low, preferred_element_type=jnp.float32)
+        cols = pl.ds(start, 2 * LANES)
+        emit(cols, both[0:padded] + both[padded : 2 * padded] + rest)
+        tail_high[:, cols] = spread(tiles, 0, own, blocks)
+        tail_low[:, cols] = spread(tiles, 1, own, blocks)
         return 0
 
-    lax.fori_loop(0, count // LANES, column, 0)
+    lax.fori_loop(0, count // (2 * LANES), step, 0)
 
 
 def picked(source, start, blocks, index, out):
@@ -107,29 +145,35 @@
     ext[padded : 2 * padded, at : at + width] = low
 
 
-def product(ext, padded, span, w_high, w_low, cols):
-    k = slice(*span)
-    both = jnp.dot(ext[:, k], w_high[k, cols], preferred_element_type=jnp.float32)
-    rest = jnp.dot(ext[0:padded, k], w_low[k, cols], preferred_element_type=jnp.float32)
+def product(ext, padded, start, w_high, w_low, cols):
+    k = slice(start, start + w_high.shape[0])
+    both = jnp.dot(ext[:, k], w_high[:, cols], preferred_element_type=jnp.float32)
+    rest = jnp.dot(ext[0:padded, k], w_low[:, cols], preferred_element_type=jnp.float32)
     return both[0:padded] + both[padded : 2 * padded] + rest
 
 
-def small(value, m_high, m_low):
+def reach(value, links, weights, start, width):
     padded = value.shape[0]
-    high, low = halves(value)
-    both = jnp.concatenate([high, low], axis=0)
-    both = jnp.dot(both, m_high, preferred_element_type=jnp.float32)
-    rest = jnp.dot(high, m_low, preferred_element_type=jnp.float32)
-    return both[0:padded] + both[padded : 2 * padded] + rest
+    rows = [value[r * SUB : (r + 1) * SUB, :] for r in range(padded // SUB)]
+    totals = [None] * len(rows)
+    for k in range(links.shape[0]):
+        link = jnp.broadcast_to(links[k : k + 1, :], (SUB, LANES))
+        weight = jnp.broadcast_to(weights[k : k + 1, :], (SUB, LANES))
+        weight = jnp.where((link >= start) & (link < start + width), weight, 0.0)
+        lane = link & (LANES - 1)
+        for r, row in enumerate(rows):
+            term = weight * jnp.take_along_axis(row, lane, axis=1)
+            totals[r] = term if totals[r] is None else totals[r] + term
+    return jnp.concatenate(totals, axis=0)
 
 
 def body(
     n_patch, n_lev, levels,
     field, sc1, sd1, sc2, sd2, pl1, pw1, ul1, uw1, pl2, pw2, ul2, uw2,
     gathered,
-    xs, ext, merged, p1h, p1l, u1h, u1l, p2h, p2l, u2h, u2l,
+    xs, ext, merged, t1h, t1l, t2h, t2l,
     det1, sm1, det2, sm2, hsend, hrecv,
-    ext2, glink, gweight, rlink, rweight, mh, ml, part, full1, full2, done,
+    ext2, glink, gweight, rlink, rweight, part, full1, full2, done, early,
     ms_sem, mr_sem,
     hs_sem, hr_sem, as_sem, ar_sem,
 ):
@@ -224,47 +268,19 @@
     e2 = n2 + 2 * halo2
     wide = 256
 
-    def predict(into, start, values, depth, w_high, w_low, n, add):
+    def add_tail(into, start, source, depth, high, low, n, add):
         for c in range(0, n, wide):
             cols = slice(start + c, start + c + wide)
-            source = ext if n1 <= w_high.shape[1] else ext2
-            got = product(source, padded, depth, w_high, w_low, cols)
-            old = values(cols)
+            got = product(source, padded, depth, high, low, cols)
+            old = into[:, cols]
             into[:, cols] = old + got if add else old - got
 
-    def fine1(cols):
-        return xs[:, cols]
-
-    def coarse1(cols):
-        return xs[:, n1 + cols.start : n1 + cols.stop]
-
-    def fine2(cols):
-        return sm1[:, cols]
-
-    def coarse2(cols):
-        return sm1[:, n2 + cols.start : n2 + cols.stop]
-
-    def held(ref):
-        return lambda cols: ref[:, cols]
-
-    h1 = 2 * halo1 // LANES
-    h2 = 2 * halo2 // LANES
     lower = lax.broadcasted_iota(jnp.int32, (padded, LANES), 1) < halo2
 
-    def tail(phase, side):
-        if phase == 2:
-            return slice(0, LANES)
-        return slice(side * LANES, (side + 1) * LANES)
-
-    def sided(phase, side, value):
-        if phase != 2:
-            return value
-        return jnp.where(lower, value, 0.0) if side == 0 else jnp.where(lower, 0.0, value)
-
-    def halo_part(phase, side, column, value):
-        cols = slice(column * LANES, (column + 1) * LANES)
-        k = tail(phase, side)
-        return small(sided(phase, side, value), mh[phase, k, cols], ml[phase, k, cols])
+    def halo_part(phase, side, value, links, weights, at):
+        width = halo2 if phase == 2 else halo1
+        start = (n2 if phase == 2 else n1) + side * width
+        return reach(value, links.at[at, phase], weights.at[at, phase], start, width)
 
     def two(send):
         return jnp.concatenate([send[0, 1:2, :], send[0, 0:1, :]], axis=1)
@@ -286,35 +302,32 @@
         for c in meta_to(side):
             c.start()
     put(ext, padded, 0, xs[:, n1:cells])
-    build(pl1, pw1, merged, p1h, p1l, 0, n1, e1 // LANES)
-    predict(det1, 0, fine1, (0, n1), p1h, p1l, n1, False)
+
+    def fine1(cols, got):
+        det1[:, cols] = xs[:, cols] - got
+
+    stage(pl1, pw1, merged, 0, n1, b1, e1 // LANES, ext, t1h, t1l, fine1)
     picked(det1, 0, b1, sd1[0, 1:2, :], part.at[0])
     picked(det1, 0, b1, sd1[0, 0:1, :], part.at[1])
 
-    def spread(links, weights, phase, column, blocks, base):
-        build(
-            links, weights, merged, mh.at[phase], ml.at[phase], 0, LANES, blocks, base,
-            column * LANES,
-        )
-
-    for side in range(2):
-        spread(glink.at[side, 0], gweight.at[side, 0], 0, side, h1, b1)
-
     def step0(side):
         copy_to(0, side).wait_recv()
-        hsend[1, side] = part[side] - halo_part(0, side, side, hrecv[0, side])
+        hsend[1, side] = part[side] - halo_part(0, side, hrecv[0, side], glink, gweight, side)
         copy_to(1, side).start()
 
     both_sides(step0)
     put(ext, padded, n1, hrecv[0, 0])
     put(ext, padded, n1 + halo1, hrecv[0, 1])
-    predict(det1, 0, held(det1), (n1, e1), p1h, p1l, n1, False)
+    add_tail(det1, 0, ext, n1, t1h, t1l, n1, False)
     scatter(det1, 0)
 
-    spread(glink.at[0, 1], gweight.at[0, 1], 1, 0, h1, b1)
-    build(ul1, uw1, merged, u1h, u1l, n2, n2, e1 // LANES)
     put(ext, padded, 0, det1[...])
-    predict(sm1, n2, coarse1, (0, n1), u1h, u1l, n2, True)
+
+    def coarse1(cols, got):
+        at = pl.ds(pl.multiple_of(cols.start + n1, LANES), cols.size)
+        sm1[:, cols] = xs[:, at] + got
+
+    stage(ul1, uw1, merged, n2, n2, b1, e1 // LANES, ext, t1h, t1l, coarse1)
     picked(sm1, n2, b2, two(sc2), part.at[0])
     picked(det1, 0, b1, sd1[0, 1:2, :], full1.at[0])
     picked(det1, 0, b1, sd1[0, 0:1, :], full1.at[1])
@@ -322,56 +335,62 @@
         for c in meta_to(side):
             c.wait_recv()
     for side in range(2):
-        spread(rlink.at[side, 0], rweight.at[side, 0], 0, 2 + side, h1, b1)
-    spread(glink.at[0, 2], gweight.at[0, 2], 2, 0, h2, b2)
-    build(pl2, pw2, merged, p2h, p2l, 0, n2, e2 // LANES)
-    for side in range(2):
-        spread(rlink.at[side, 1], rweight.at[side, 1], 1, 2 + side, h1, b1)
+        early[side] = halo_part(0, 1 - side, hsend[0, 1 - side], rlink, rweight, side)
 
     def step1(side):
         copy_to(1, side).wait_recv()
-        value = hrecv[1, side] - halo_part(0, 1 - side, 2 + side, hsend[0, 1 - side])
+        value = hrecv[1, side] - early[side]
         done[side] = value
-        hsend[2, side] = part[0] + halo_part(1, side, 0, value)
+        hsend[2, side] = part[0] + halo_part(1, side, value, glink, gweight, 0)
         copy_to(2, side).start()
 
     both_sides(step1)
     put(ext, padded, n1, done[0])
     put(ext, padded, n1 + halo1, done[1])
-    predict(sm1, n2, held(sm1), (n1, e1), u1h, u1l, n2, True)
-
-    build(ul1, uw1, merged, u1h, u1l, 0, n2, e1 // LANES)
-    predict(sm1, 0, coarse1, (0, e1), u1h, u1l, n2, True)
+    add_tail(sm1, n2, ext, n1, t1h, t1l, n2, True)
     put(ext2, padded, 0, sm1[:, n2:n1])
+
+    stage(ul1, uw1, merged, 0, n2, b1, e1 // LANES, ext, t1h, t1l, coarse1)
+    add_tail(sm1, 0, ext, n1, t1h, t1l, n2, True)
+
+    def fine2(cols, got):
+        det2[:, cols] = sm1[:, cols] - got
+
+    stage(pl2, pw2, merged, 0, n2, b2, e2 // LANES, ext2, t2h, t2l, fine2)
     picked(sm1, n2, b2, two(sc2), full2)
-    predict(det2, 0, fine2, (0, n2), p2h, p2l, n2, False)
     picked(det2, 0, b2, two(sd2), part.at[1])
+    for side in range(2):
+        early[side] = halo_part(1, 1 - side, full1[1 - side], rlink, rweight, side)
 
     def step2(side):
         copy_to(2, side).wait_recv()
-        value = hrecv[2, side] + halo_part(1, 1 - side, 2 + side, full1[1 - side])
+        value = hrecv[2, side] + early[side]
         done[side] = value
-        hsend[3, side] = part[1] - halo_part(2, side, 0, value)
+        hsend[3, side] = part[1] - halo_part(2, side, value, glink, gweight, 0)
         copy_to(3, side).start()
 
     both_sides(step2)
     put(ext2, padded, n2, jnp.where(lower, done[0], done[1]))
-    predict(det2, 0, held(det2), (n2, e2), p2h, p2l, n2, False)
+    add_tail(det2, 0, ext2, n2, t2h, t2l, n2, False)
     scatter(det2, n1)
 
     put(ext2, padded, 0, det2[...])
-    for side in range(2):
-        spread(rlink.at[side, 2], rweight.at[side, 2], 2, 2 + side, h2, b2)
-    build(ul2, uw2, merged, u2h, u2l, 0, n2, e2 // LANES)
-    predict(sm2, 0, coarse2, (0, n2), u2h, u2l, n2, True)
+
+    def coarse2(cols, got):
+        at = pl.ds(pl.multiple_of(cols.start + n2, LANES), cols.size)
+        sm2[:, cols] = sm1[:, at] + got
+
+    stage(ul2, uw2, merged, 0, n2, b2, e2 // LANES, ext2, t2h, t2l, coarse2)
+    for side in range(2):
+        early[side] = halo_part(2, 1 - side, full2[...], rlink, rweight, side)
 
     def step3(side):
         copy_to(3, side).wait_recv()
-        done[side] = hrecv[3, side] - halo_part(2, 1 - side, 2 + side, full2[...])
+        done[side] = hrecv[3, side] - early[side]
 
     both_sides(step3)
     put(ext2, padded, n2, jnp.where(lower, done[0], done[1]))
-    predict(sm2, 0, held(sm2), (n2, e2), u2h, u2l, n2, True)
+    add_tail(sm2, 0, ext2, n2, t2h, t2l, n2, True)
     scatter(sm2, n1 + n2)
 
     for s in range(n_lev):
@@ -433,15 +452,11 @@
         scratch_shapes=[
             pltpu.VMEM((padded, cells), f32),
             pltpu.VMEM((2 * padded, e1), bf16),
-            pltpu.VMEM((slots, -(-(e1 // LANES) // SUB) * SUB, LANES), f32),
-            pltpu.VMEM((e1, n1), bf16),
-            pltpu.VMEM((e1, n1), bf16),
-            pltpu.VMEM((e1, n1), bf16),
-            pltpu.VMEM((e1, n1), bf16),
-            pltpu.VMEM((e2, n2), bf16),
-            pltpu.VMEM((e2, n2), bf16),
-            pltpu.VMEM((e2, n2), bf16),
-            pltpu.VMEM((e2, n2), bf16),
+            pltpu.VMEM((2, slots, -(-(e1 // LANES) // SUB) * SUB, LANES), f32),
+            pltpu.VMEM((e1 - n1, n1), bf16),
+            pltpu.VMEM((e1 - n1, n1), bf16),
+            pltpu.VMEM((e2 - n2, n2), bf16),
+            pltpu.VMEM((e2 - n2, n2), bf16),
             pltpu.VMEM((padded, n1), f32),
             pltpu.VMEM((padded, n1), f32),
             pltpu.VMEM((padded, n2), f32),
@@ -453,11 +468,10 @@
             pltpu.VMEM((2, 3, slots, LANES), f32),
             pltpu.VMEM((2, 3, slots, LANES), jnp.int32),
             pltpu.VMEM((2, 3, slots, LANES), f32),
-            pltpu.VMEM((3, 2 * LANES, 4 * LANES), bf16),
-            pltpu.VMEM((3, 2 * LANES, 4 * LANES), bf16),
             pltpu.VMEM((2, padded, LANES), f32),
             pltpu.VMEM((2, padded, LANES), f32),
             pltpu.VMEM((padded, LANES), f32),
+            pltpu.VMEM((2, padded, LANES), f32),
             pltpu.VMEM((2, padded, LANES), f32),
             pltpu.SemaphoreType.DMA((2, 2)),
             pltpu.SemaphoreType.DMA((2, 2)),

time: 30.3 us -> 27.4 us (0.904)
  Pallas kernels: 30.1 us -> 27.2 us
    pallas_call x1, Pallas kernels: 27.7 us -> 24.7 us  [on_device(): pl.pallas_call(functools.partial(body, n_patch, n_lev, levels), out_shape...]
where the time goes in v1:
time: 27.4 us; the launch traced here: 27.2 us
  Pallas kernels  27.2 us (99%)
    pallas_call x1, Pallas kernels, on_device(): pl.pallas_call(functools.partial(body, n_patch, n_lev, levels), out_shape...  24.7 us
    pallas_call x1, Pallas kernels, on_device(): pl.pallas_call(transform, out_shape=jax.ShapeDtypeStruct((tracers, levels...  2.46 us

profile of v1, /device:TPU:0, one launch (start us, length us, event | category | flops | bytes accessed | tf_op | source)
XLA Modules:
  0.0 27.2 jit_solution(15510039345100966948)
XLA Ops:
  0.0 24.7 %shard_map.145.gathered = f32[4,64,512]{2,1,0:T(8,128)} custom-call(f32[3,20,2048]{2,1,0:T(8,128)} %bitcast.2, s32[1,2,128]{2,1,0:T(2,128)} %sc1.1, s32[1,2,128]{2,1,0:T(2,128)} %sd1.1, s32[1,2,64]{2,1,0:T(2,128)} %sc2.1, s32[1,2,64]{2,1,0:T(2,128)} %sd2.1, s32[8,1024]{1,0:T(8,128)} %pl1.1, f32[8,1024]{1,0:T(8,128)} %pw1.1, s32[8,1024]{1,0:T(8,128)} %ul1.1, ...), custom_call_target="tpu_custom_call" | custom-call | tf_op jit(solution)/shard_map/pallas_call | solution.py:447
  24.8 2.5 %shard_map.146 = f32[3,80,512]{2,1,0:T(8,128)} custom-call(f32[4,64,512]{2,1,0:T(8,128)} %shard_map.145.gathered, bf16[240,256]{1,0:T(8,128)(2,1)} %constant.4.clone.t_high, bf16[240,256]{1,0:T(8,128)(2,1)} %constant.5.clone.t_low), custom_call_target="tpu_custom_call" | custom-call | tf_op jit(solution)/shard_map/pallas_call | solution.py:485

commit v2 on v1

--- a/solution.py
+++ b/solution.py
@@ -169,14 +169,17 @@
 
 def body(
     n_patch, n_lev, levels,
-    field, sc1, sd1, sc2, sd2, pl1, pw1, ul1, uw1, pl2, pw2, ul2, uw2,
-    gathered,
+    *refs,
+):
+    given, gathered, held, rest = refs[:13], refs[13], refs[14:27], refs[27:]
+    field, sc1, sd1, sc2, sd2, pl1, pw1, ul1, uw1, pl2, pw2, ul2, uw2 = held
+    (
     xs, ext, merged, t1h, t1l, t2h, t2l,
     det1, sm1, det2, sm2, hsend, hrecv,
     ext2, glink, gweight, rlink, rweight, part, full1, full2, done, early,
     ms_sem, mr_sem,
-    hs_sem, hr_sem, as_sem, ar_sem,
-):
+    hs_sem, hr_sem, as_sem, ar_sem, in_sem,
+    ) = rest
     tracers, own, cells = field.shape
     rows = own * tracers
     padded = xs.shape[0]
@@ -198,11 +201,27 @@
             barrier, inc=1, device_id={"lev": lax.rem(me + d, n_lev)}, device_id_type=MESH
         )
 
-    if padded > rows:
-        edge = rows // SUB * SUB
-        xs[edge:padded, :] = jnp.zeros((padded - edge, cells), jnp.float32)
-    for t in range(tracers):
-        xs[t * own : (t + 1) * own, :] = field[t]
+    coarse = (slice(None), slice(None), slice(n1, cells))
+    fine = (slice(None), slice(None), slice(0, n1))
+    loads = {0: pltpu.make_async_copy(given[0].at[coarse], field.at[coarse], in_sem.at[0])}
+    for i in (1, 5, 6, 2):
+        loads[i] = pltpu.make_async_copy(given[i], held[i], in_sem.at[i])
+    loads[13] = pltpu.make_async_copy(given[0].at[fine], field.at[fine], in_sem.at[13])
+    for i in (3, 4, 7, 8, 9, 10, 11, 12):
+        loads[i] = pltpu.make_async_copy(given[i], held[i], in_sem.at[i])
+    for load in loads.values():
+        load.start()
+
+    def pack(start, stop):
+        if padded > rows:
+            edge = rows // SUB * SUB
+            xs[edge:padded, start:stop] = jnp.zeros((padded - edge, stop - start), jnp.float32)
+        for t in range(tracers):
+            xs[t * own : (t + 1) * own, start:stop] = field[t, :, start:stop]
+
+    loads.pop(0).wait()
+    loads.pop(1).wait()
+    pack(n1, cells)
 
     def copy_to(phase, side):
         return pltpu.make_async_remote_copy(
@@ -295,6 +314,9 @@
     pl.semaphore_wait(barrier, 2 + n_lev - 1)
     for side in range(2):
         copy_to(0, side).start()
+    for load in loads.values():
+        load.wait()
+    pack(0, n1)
     share(0, pl1, pw1, 0, b1, (sd1[0, 1:2, :], sd1[0, 0:1, :]))
     share(1, ul1, uw1, n2, b2, (two(sc2), two(sc2)))
     share(2, pl2, pw2, 0, b2, (two(sd2), two(sd2)))
@@ -447,9 +469,11 @@
     gathered = pl.pallas_call(
         functools.partial(body, n_patch, n_lev, levels),
         out_shape=jax.ShapeDtypeStruct((n_lev, padded, chunk), f32),
-        in_specs=[pl.BlockSpec(memory_space=pltpu.VMEM)] * 13,
+        in_specs=[pl.BlockSpec(memory_space=pltpu.HBM)] * 13,
         out_specs=pl.BlockSpec(memory_space=pltpu.VMEM),
         scratch_shapes=[
+            pltpu.VMEM((tracers, own, cells), f32),
+            *(pltpu.VMEM(a.shape, a.dtype) for a in args[1:]),
             pltpu.VMEM((padded, cells), f32),
             pltpu.VMEM((2 * padded, e1), bf16),
             pltpu.VMEM((2, slots, -(-(e1 // LANES) // SUB) * SUB, LANES), f32),
@@ -479,14 +503,18 @@
             pltpu.SemaphoreType.DMA((4, 2)),
             pltpu.SemaphoreType.DMA((n_lev,)),
             pltpu.SemaphoreType.DMA((n_lev,)),
+            pltpu.SemaphoreType.DMA((14,)),
         ],
-        compiler_params=pltpu.CompilerParams(collective_id=0, has_side_effects=True),
-    )(jnp.transpose(field, (1, 0, 2)), *args[1:])
+        compiler_params=pltpu.CompilerParams(
+            collective_id=0, has_side_effects=True, vmem_limit_bytes=16 << 20
+        ),
+    )(*(pltpu.with_memory_space_constraint(a, pltpu.HBM) for a in (jnp.transpose(field, (1, 0, 2)), *args[1:])))
     result = pl.pallas_call(
         transform,
         out_shape=jax.ShapeDtypeStruct((tracers, levels, chunk), f32),
         in_specs=[pl.BlockSpec(memory_space=pltpu.VMEM)] * 3,
         out_specs=pl.BlockSpec(memory_space=pltpu.VMEM),
+        compiler_params=pltpu.CompilerParams(vmem_limit_bytes=8 << 20),
     )(gathered, jnp.asarray(t_high), jnp.asarray(t_low))
     return jnp.transpose(result, (1, 0, 2))
 

time: 27.4 us -> 24.4 us (0.89)
  Pallas kernels: 27.2 us -> 24.3 us
    pallas_call x1, Pallas kernels: 24.7 us -> 22.9 us  [on_device(): pl.pallas_call(functools.partial(body, n_patch, n_lev, levels), out_shape...]
    pallas_call x1, Pallas kernels: 2.46 us -> 1.34 us  [on_device(): pl.pallas_call(transform, out_shape=jax.ShapeDtypeStruct((tracers, levels...]
where the time goes in v2:
time: 24.4 us; the launch traced here: 24.3 us
  Pallas kernels  24.3 us (100%)
    pallas_call x1, Pallas kernels, on_device(): pl.pallas_call(functools.partial(body, n_patch, n_lev, levels), out_shape...  22.9 us
    pallas_call x1, Pallas kernels, on_device(): pl.pallas_call(transform, out_shape=jax.ShapeDtypeStruct((tracers, levels...  1.34 us

profile of v2, /device:TPU:0, one launch (start us, length us, event | category | flops | bytes accessed | tf_op | source)
XLA Modules:
  0.0 24.3 jit_solution(3492442208451668479)
XLA Ops:
  0.0 0.0 copy-start
  0.0 0.0 copy-start.1
  0.0 22.9 %shard_map.145.gathered = f32[4,64,512]{2,1,0:T(8,128)S(1)} custom-call(f32[3,20,2048]{2,1,0:T(8,128)} %bitcast.2, s32[1,2,128]{2,1,0:T(2,128)} %refs_1_.1, s32[1,2,128]{2,1,0:T(2,128)} %refs_2_.1, s32[1,2,64]{2,1,0:T(2,128)} %refs_3_.1, s32[1,2,64]{2,1,0:T(2,128)} %refs_4_.1, s32[8,1024]{1,0:T(8,128)} %refs_5_.1, f32[8,1024]{1,0:T(8,128)} %refs_6_.1, ...), custom_call_target="tpu_custom_call" | custom-call | tf_op jit(solution)/shard_map/pallas_call | solution.py:469
  22.9 0.0 copy-done
  22.9 0.0 copy-done.1
  23.0 1.3 %shard_map.146 = f32[3,80,512]{2,1,0:T(8,128)} custom-call(f32[4,64,512]{2,1,0:T(8,128)S(1)} %shard_map.145.gathered, bf16[240,256]{1,0:T(8,128)(2,1)S(1)} %copy-done.1, bf16[240,256]{1,0:T(8,128)(2,1)S(1)} %copy-done), custom_call_target="tpu_custom_call" | custom-call | tf_op jit(solution)/shard_map/pallas_call | solution.py:512
Async XLA Ops:
  0.0 22.9 %copy-start = (bf16[240,256]{1,0:T(8,128)(2,1)S(1)}, bf16[240,256]{1,0:T(8,128)(2,1)}, u32[]{:S(2)}) copy-start(bf16[240,256]{1,0:T(8,128)(2,1)} %constant.5.clone.t_low) | copy-start | bytes 368644
  0.0 22.9 %copy-start.1 = (bf16[240,256]{1,0:T(8,128)(2,1)S(1)}, bf16[240,256]{1,0:T(8,128)(2,1)}, u32[]{:S(2)}) copy-start(bf16[240,256]{1,0:T(8,128)(2,1)} %constant.4.clone.t_high) | copy-start | bytes 368644

commit v3 on v2

v3 whole, which is shorter than its diff:
```python
import functools

import jax
import jax.numpy as jnp
import ml_dtypes
import numpy as np
from jax import lax
from jax.experimental import pallas as pl
from jax.experimental.pallas import tpu as pltpu
from jax.sharding import PartitionSpec as P

LANES = 128
SUB = 8
MESH = pl.DeviceIdType.MESH


def cosine_table(length):
    rows = np.arange(length, dtype=np.float64)[:, None]
    columns = np.arange(length, dtype=np.float64)[None, :]
    matrix = np.cos(np.pi * (columns + 0.5) * rows / length) * np.sqrt(2.0 / length)
    matrix[0] *= np.sqrt(0.5)
    return matrix


def spread_table(levels, tracers, groups, padded):
    own = levels // groups
    table = cosine_table(levels).reshape(levels, groups, own)
    wide = np.zeros((tracers, levels, groups, padded))
    for t in range(tracers):
        wide[t, :, :, t * own : (t + 1) * own] = table
    wide = wide.reshape(levels * tracers, groups * padded).astype(np.float32)
    high = wide.astype(ml_dtypes.bfloat16)
    low = (wide - high.astype(np.float32)).astype(ml_dtypes.bfloat16)
    return high, low


def halves(x):
    high = x.astype(jnp.bfloat16)
    low = (x - high.astype(jnp.float32)).astype(jnp.bfloat16)
    return high, low


def along(table, index):
    numbers = lax.GatherDimensionNumbers(
        offset_dims=(),
        collapsed_slice_dims=(0,),
        start_index_map=(0,),
        operand_batching_dims=(1,),
        start_indices_batching_dims=(1,),
    )
    mode = lax.GatherScatterMode.PROMISE_IN_BOUNDS
    return lax.gather(table, index[:, :, None], numbers, (1, 1), mode=mode)


def tile(links, weights, merged, cols, blocks):
    slots = links.shape[0]
    lane = []
    block = []
    weight = []
    for k in range(slots):
        link = jnp.broadcast_to(links[k : k + 1, cols], (SUB, LANES))
        lane.append(link & (LANES - 1))
        block.append(link >> 7)
        weight.append(jnp.broadcast_to(weights[k : k + 1, cols], (SUB, LANES)))
    which = lax.broadcasted_iota(jnp.int32, (SUB, LANES), 0)
    same = [[lane[j] == lane[k] for j in range(k)] for k in range(slots)]
    for g in range(-(-blocks // SUB)):
        placed = []
        for k in range(slots):
            mine = jnp.where(block[k] == which + g * SUB, weight[k], 0.0)
            total = mine
            for j in range(k):
                total = total + jnp.where(same[k][j], placed[j], 0.0)
            placed.append(mine)
            merged[k, g * SUB : (g + 1) * SUB, :] = total
    none = jnp.zeros((2 * SUB - slots, LANES), jnp.float32)
    tables = [halves(jnp.concatenate([merged[:, b, :], none], axis=0)) for b in range(blocks)]
    short = [jnp.concatenate([v, v], axis=0).astype(jnp.int16) for v in lane]
    strips = []
    for s in range(LANES // (2 * SUB)):
        rows = lax.broadcasted_iota(jnp.int16, (2 * SUB, LANES), 0) + jnp.int16(s * 2 * SUB)
        index = jnp.full((2 * SUB, LANES), slots, jnp.int16)
        for k in range(slots):
            index = jnp.where(short[k] == rows, jnp.int16(k), index)
        strips.append(index)
    return tables, strips


def spread(tiles, part, first, last):
    return jnp.concatenate(
        [
            jnp.concatenate(
                [along(tables[b][part], index) for b in range(first, last) for index in strips],
                axis=0,
            )
            for tables, strips in tiles
        ],
        axis=1,
    )


def stage(links, weights, merged, first, count, own, blocks, ext, tail, emit):
    padded = ext.shape[0] // 2
    depth = own * LANES
    width = min(count, 2 * LANES)

    def step(t, _):
        start = pl.multiple_of(first + t * width, width)
        tiles = [
            tile(
                links, weights, merged.at[h],
                pl.ds(pl.multiple_of(start + h * LANES, LANES), LANES), blocks,
            )
            for h in range(width // LANES)
        ]
        high = spread(tiles, 0, 0, own)
        low = spread(tiles, 1, 0, own)
        both = jnp.dot(ext[:, 0:depth], high, preferred_element_type=jnp.float32)
        rest = jnp.dot(ext[0:padded, 0:depth], low, preferred_element_type=jnp.float32)
        cols = pl.ds(start, width)
        emit(cols, both[0:padded] + both[padded : 2 * padded] + rest)
        if tail is not None:
            tail[0][:, cols] = spread(tiles, 0, own, blocks)
            tail[1][:, cols] = spread(tiles, 1, own, blocks)
        return 0

    lax.fori_loop(0, count // width, step, 0)


def prepare(links, weights, merged, count, blocks, out):
    def step(t, _):
        cols = pl.ds(pl.multiple_of(t * LANES, LANES), LANES)
        tiles = [tile(links, weights, merged.at[0], cols, blocks)]
        out[0][:, cols] = spread(tiles, 0, 0, blocks)
        out[1][:, cols] = spread(tiles, 1, 0, blocks)
        return 0

    lax.fori_loop(0, count // LANES, step, 0)


def picked(source, start, blocks, index, out):
    lane = jnp.broadcast_to(index & (LANES - 1), (SUB, LANES))
    block = jnp.broadcast_to(index >> 7, (SUB, LANES))
    for r in range(source.shape[0] // SUB):
        rows = slice(r * SUB, (r + 1) * SUB)
        got = None
        for b in range(blocks):
            cols = slice(start + b * LANES, start + (b + 1) * LANES)
            t = jnp.take_along_axis(source[rows, cols], lane, axis=1)
            got = t if got is None else jnp.where(block == b, t, got)
        out[rows, :] = got


def put(ext, padded, at, value):
    high, low = halves(value)
    width = value.shape[1]
    ext[0:padded, at : at + width] = high
    ext[padded : 2 * padded, at : at + width] = low


def product(ext, padded, start, w_high, w_low, cols):
    k = slice(start, start + w_high.shape[0])
    both = jnp.dot(ext[:, k], w_high[:, cols], preferred_element_type=jnp.float32)
    rest = jnp.dot(ext[0:padded, k], w_low[:, cols], preferred_element_type=jnp.float32)
    return both[0:padded] + both[padded : 2 * padded] + rest


def reach(value, links, weights, keep):
    padded = value.shape[0]
    rows = [value[r * SUB : (r + 1) * SUB, :] for r in range(padded // SUB)]
    totals = [None] * len(rows)
    for k in range(links.shape[0]):
        link = jnp.broadcast_to(links[k : k + 1, :], (SUB, LANES))
        weight = jnp.broadcast_to(weights[k : k + 1, :], (SUB, LANES))
        weight = jnp.where(keep(link), weight, 0.0)
        lane = link & (LANES - 1)
        for r, row in enumerate(rows):
            term = weight * jnp.take_along_axis(row, lane, axis=1)
            totals[r] = term if totals[r] is None else totals[r] + term
    return jnp.concatenate(totals, axis=0)


def body(n_patch, n_lev, levels, *refs):
    given, gathered, held, rest = refs[:13], refs[13], refs[14:27], refs[27:]
    field, sc1, sd1, sc2, sd2, pl1, pw1, ul1, uw1, pl2, pw2, ul2, uw2 = held
    (
        xs, ext, ext2, merged, t1h, t1l, t2h, t2l, w2h, w2l,
        det1, sm1, det2, sm2,
        asend, arecv, afar, bsend, brecv, csend, crecv, cfar,
        link1, weight1, link2, weight2, link3, weight3, rlink1, rweight1, rlink2, rweight2,
        fpart, own2, early1, early2, hsend, hrecv,
        in_sem, x_send, x_recv, m_send, m_recv, g_send, g_recv, h_send, h_recv,
    ) = rest
    tracers, own, cells = field.shape
    rows = own * tracers
    padded = xs.shape[0]
    n1 = cells // 2
    n2 = cells // 4
    halo1 = sc1.shape[2]
    halo2 = sc2.shape[2]
    chunk = cells // n_lev
    b1 = n1 // LANES
    b2 = n2 // LANES
    e1 = n1 + 2 * halo1
    e2 = n2 + 2 * halo2
    wide = 256
    me = lax.axis_index("lev")
    patch = lax.axis_index("patch")

    def away(steps):
        return lax.rem(patch + n_patch + steps, n_patch)

    barrier = pltpu.get_barrier_semaphore()
    for steps in (-2, -1, 1, 2):
        pl.semaphore_signal(barrier, inc=1, device_id={"patch": away(steps)}, device_id_type=MESH)
    for d in range(1, n_lev):
        pl.semaphore_signal(
            barrier, inc=1, device_id={"lev": lax.rem(me + d, n_lev)}, device_id_type=MESH
        )

    coarse = (slice(None), slice(None), slice(n1, cells))
    fine = (slice(None), slice(None), slice(0, n1))
    loads = {0: pltpu.make_async_copy(given[0].at[coarse], field.at[coarse], in_sem.at[0])}
    for i in (1, 5, 6, 2):
        loads[i] = pltpu.make_async_copy(given[i], held[i], in_sem.at[i])
    loads[13] = pltpu.make_async_copy(given[0].at[fine], field.at[fine], in_sem.at[13])
    for i in (3, 4, 7, 8, 9, 10, 11, 12):
        loads[i] = pltpu.make_async_copy(given[i], held[i], in_sem.at[i])
    for load in loads.values():
        load.start()

    def loaded(*which):
        for i in which:
            loads[i].wait()

    def pack(start, stop):
        if padded > rows:
            edge = rows // SUB * SUB
            xs[edge:padded, start:stop] = jnp.zeros((padded - edge, stop - start), jnp.float32)
        for t in range(tracers):
            xs[t * own : (t + 1) * own, start:stop] = field[t, :, start:stop]

    def message(which, side, steps, source, target):
        return pltpu.make_async_remote_copy(
            src_ref=source.at[side],
            dst_ref=target.at[side],
            send_sem=x_send.at[which, side],
            recv_sem=x_recv.at[which, side],
            device_id={"patch": away(-steps if side else steps)},
            device_id_type=MESH,
        )

    near1 = [message(0, side, 1, asend, arecv) for side in range(2)]
    far1 = [message(1, side, 2, asend, afar) for side in range(2)]
    part1 = [message(2, side, 1, bsend, brecv) for side in range(2)]
    near2 = [message(3, side, 1, csend, crecv) for side in range(2)]
    far2 = [message(4, side, 2, csend, cfar) for side in range(2)]

    def meta(which, side, source, target):
        return pltpu.make_async_remote_copy(
            src_ref=source,
            dst_ref=target.at[side],
            send_sem=m_send.at[which, side],
            recv_sem=m_recv.at[which, side],
            device_id={"patch": away(-1 if side else 1)},
            device_id_type=MESH,
        )

    def half(ref, side):
        return ref.at[:, side * LANES : (side + 1) * LANES]

    meta1 = [meta(0, side, half(link1, side), rlink1) for side in range(2)]
    meta1 += [meta(1, side, half(weight1, side), rweight1) for side in range(2)]
    meta2 = [meta(2, side, link2, rlink2) for side in range(2)]
    meta2 += [meta(3, side, weight2, rweight2) for side in range(2)]

    outgoing = []

    def scatter(source, base):
        for piece in range(source.shape[1] // chunk):
            d = base // chunk + piece
            part = source.at[:, piece * chunk : (piece + 1) * chunk]
            copy = pltpu.make_async_remote_copy(
                src_ref=part,
                dst_ref=gathered.at[me],
                send_sem=g_send.at[d],
                recv_sem=g_recv.at[me],
                device_id={"lev": d},
                device_id_type=MESH,
            )
            outgoing.append((d, copy))

            @pl.when(me != d)
            def _():
                copy.start()

            @pl.when(me == d)
            def _():
                gathered[d] = part[...]

    def add_tail(into, n, tail, add):
        for c in range(0, n, wide):
            cols = slice(c, c + wide)
            got = product(ext, padded, n1, *tail, cols)
            old = into[:, cols]
            into[:, cols] = old + got if add else old - got

    lower = lax.broadcasted_iota(jnp.int32, (padded, LANES), 1) < halo2
    first = lax.broadcasted_iota(jnp.int32, (SUB, LANES), 1) < halo2

    def two(send):
        return jnp.concatenate([send[0, 1:2, :], send[0, 0:1, :]], axis=1)

    def side1(side):
        start = n1 + side * halo1
        return lambda link: (link >= start) & (link < start + halo1)

    def side2(same):
        def keep(link):
            ours = (link < n2 + halo2) == first
            return (link >= n2) & (ours if same else ~ours)

        return keep

    loaded(0, 1)
    pack(n1, cells)
    for side in range(2):
        picked(xs, n1, b1, sc1[0, 1 - side : 2 - side, :], asend.at[side])
    pl.semaphore_wait(barrier, 4 + n_lev - 1)
    for side in range(2):
        near1[side].start()
        far1[side].start()

    loaded(2, 5, 6, 13)
    put(ext, padded, 0, xs[:, n1:cells])
    pack(0, n1)
    for side in range(2):
        index = sd1[0, 1 - side : 2 - side, :]
        picked(pl1, 0, b1, index, half(link1, side))
        picked(pw1, 0, b1, index, half(weight1, side))
        picked(xs, 0, b1, index, fpart.at[side])

    def sent1(cols, got):
        for side in range(2):
            bsend[side] = fpart[side] - got[:, side * LANES : (side + 1) * LANES]

    stage(link1, weight1, merged, 0, 2 * LANES, b1, b1, ext, None, sent1)
    for copy in part1 + meta1:
        copy.start()

    def fine1(cols, got):
        det1[:, cols] = xs[:, cols] - got

    tail1 = (t1h, t1l)
    stage(pl1, pw1, merged, 0, n1, b1, e1 // LANES, ext, tail1, fine1)

    loaded(3, 4, 7, 8, 9, 10, 11, 12)
    picked(pl2, 0, b2, two(sd2), link2)
    picked(pw2, 0, b2, two(sd2), weight2)
    for copy in meta2:
        copy.start()

    for side in range(2):
        near1[side].wait_recv()
        put(ext, padded, n1 + side * halo1, arecv[side])
    add_tail(det1, n1, tail1, False)
    scatter(det1, 0)
    put(ext, padded, 0, det1[...])

    def coarse1(cols, got):
        at = pl.ds(pl.multiple_of(cols.start + n1, LANES), cols.size)
        sm1[:, cols] = xs[:, at] + got

    stage(ul1, uw1, merged, 0, n1, b1, e1 // LANES, ext, tail1, coarse1)
    for copy in meta1:
        copy.wait_recv()
    for side in range(2):
        early1[side] = reach(asend[1 - side], rlink1.at[side], rweight1.at[side], side1(1 - side))
    for side in range(2):
        far1[side].wait_recv()
        part1[side].wait_recv()
        value = brecv[side] - early1[side]
        value = value - reach(afar[side], rlink1.at[side], rweight1.at[side], side1(side))
        put(ext, padded, n1 + side * halo1, value)
    add_tail(sm1, n1, tail1, True)

    put(ext2, padded, 0, sm1[:, n2:n1])
    picked(sm1, n2, b2, two(sc2), own2)
    picked(sm1, 0, b2, two(sd2), fpart.at[0])

    def sent2(cols, got):
        part = pltpu.roll(fpart[0] - got, halo2, axis=1)
        csend[0] = jnp.where(lower, own2[...], part)
        csend[1] = jnp.where(lower, part, own2[...])

    stage(link2, weight2, merged, 0, LANES, b2, b2, ext2, None, sent2)
    for side in range(2):
        near2[side].start()
        far2[side].start()

    def fine2(cols, got):
        det2[:, cols] = sm1[:, cols] - got

    tail2 = (t2h, t2l)
    stage(pl2, pw2, merged, 0, n2, b2, e2 // LANES, ext2, tail2, fine2)
    scatter(det2, n1)

    prepare(ul2, uw2, merged, n2, e2 // LANES, (w2h, w2l))
    for copy in meta2:
        copy.wait_recv()
    turned = lax.broadcasted_iota(jnp.int32, (rlink2.shape[1], LANES), 1) < halo2
    link3[...] = jnp.where(turned, rlink2[0], rlink2[1])
    weight3[...] = jnp.where(turned, rweight2[0], rweight2[1])
    early2[...] = reach(own2[...], link3, weight3, side2(False))

    for side in range(2):
        near2[side].wait_recv()
    edge = jnp.where(lower, crecv[0], crecv[1])
    hsend[...] = edge

    forward = []
    for piece in range(n2 // chunk):
        d = n1 // chunk + piece
        copy = pltpu.make_async_remote_copy(
            src_ref=hsend,
            dst_ref=hrecv.at[me],
            send_sem=h_send.at[piece],
            recv_sem=h_recv.at[me],
            device_id={"lev": d},
            device_id_type=MESH,
        )
        forward.append((d, copy))

        @pl.when(me != d)
        def _():
            copy.start()

        @pl.when(me == d)
        def _():
            hrecv[d] = edge

    put(ext2, padded, n2, edge)
    for c in range(0, n2, wide):
        cols = slice(c, c + wide)
        value = det2[:, cols] - product(ext2, padded, n2, *tail2, cols)
        put(ext2, padded, c, value)

    for side in range(2):
        far2[side].wait_recv()
    value = pltpu.roll(jnp.where(lower, crecv[1], crecv[0]), halo2, axis=1) - early2[...]
    outer = jnp.where(lower, cfar[0], cfar[1])
    put(ext2, padded, n2, value - reach(outer, link3, weight3, side2(True)))
    for c in range(0, n2, wide):
        cols = slice(c, c + wide)
        sm2[:, cols] = sm1[:, n2 + c : n2 + c + wide] + product(ext2, padded, 0, w2h, w2l, cols)
    scatter(sm2, n1 + n2)

    for s in range(n_lev):

        @pl.when(me != s)
        def _():
            pltpu.make_async_remote_copy(
                src_ref=gathered.at[s],
                dst_ref=gathered.at[s],
                send_sem=g_send.at[s],
                recv_sem=g_recv.at[s],
                device_id={"lev": s},
                device_id_type=MESH,
            ).wait_recv()

    inner = (me >= n1 // chunk) & (me < (n1 + n2) // chunk)

    @pl.when(inner)
    def _():
        for s in range(n_lev):

            @pl.when(me != s)
            def _():
                pltpu.make_async_remote_copy(
                    src_ref=hrecv.at[s],
                    dst_ref=hrecv.at[s],
                    send_sem=h_send.at[0],
                    recv_sem=h_recv.at[s],
                    device_id={"lev": s},
                    device_id_type=MESH,
                ).wait_recv()

        at = pl.multiple_of((me - n1 // chunk) * chunk, LANES)
        cols = pl.ds(at, chunk)
        for s in range(n_lev):
            high, low = halves(hrecv[s])
            both = jnp.concatenate([high, low], axis=0)
            both = jnp.dot(both, t2h[:, cols], preferred_element_type=jnp.float32)
            rest = jnp.dot(high, t2l[:, cols], preferred_element_type=jnp.float32)
            gathered[s] = gathered[s] - (both[0:padded] + both[padded : 2 * padded] + rest)

    for group in (near1, far1, part1, near2, far2, meta1, meta2):
        for copy in group:
            copy.wait_send()
    for d, copy in outgoing + forward:

        @pl.when(me != d)
        def _():
            copy.wait_send()


def transform(gathered, t_high, t_low, out):
    groups, padded, chunk = gathered.shape
    tracers, levels, _ = out.shape
    high, low = halves(gathered[...].reshape(groups * padded, chunk))
    for t in range(tracers):
        rows = slice(t * levels, (t + 1) * levels)
        out[t] = (
            jnp.dot(t_high[rows, :], high, preferred_element_type=jnp.float32)
            + jnp.dot(t_high[rows, :], low, preferred_element_type=jnp.float32)
            + jnp.dot(t_low[rows, :], high, preferred_element_type=jnp.float32)
        )


def on_device(n_patch, n_lev, *args):
    field, sc1 = args[0], args[1]
    own, tracers, cells = field.shape
    levels = own * n_lev
    rows = own * tracers
    padded = -(-rows // (2 * SUB)) * (2 * SUB)
    n1, n2 = cells // 2, cells // 4
    e1 = n1 + 2 * sc1.shape[2]
    e2 = n2 + 2 * args[3].shape[2]
    chunk = cells // n_lev
    slots = args[5].shape[0]
    t_high, t_low = spread_table(levels, tracers, n_lev, padded)
    f32, bf16 = jnp.float32, jnp.bfloat16
    gathered = pl.pallas_call(
        functools.partial(body, n_patch, n_lev, levels),
        out_shape=jax.ShapeDtypeStruct((n_lev, padded, chunk), f32),
        in_specs=[pl.BlockSpec(memory_space=pltpu.HBM)] * 13,
        out_specs=pl.BlockSpec(memory_space=pltpu.VMEM),
        scratch_shapes=[
            pltpu.VMEM((tracers, own, cells), f32),
            *(pltpu.VMEM(a.shape, a.dtype) for a in args[1:]),
            pltpu.VMEM((padded, cells), f32),
            pltpu.VMEM((2 * padded, e1), bf16),
            pltpu.VMEM((2 * padded, e2), bf16),
            pltpu.VMEM((2, slots, -(-(e1 // LANES) // SUB) * SUB, LANES), f32),
            *[pltpu.VMEM((e1 - n1, n1), bf16)] * 2,
            *[pltpu.VMEM((e2 - n2, n2), bf16)] * 2,
            *[pltpu.VMEM((e2, n2), bf16)] * 2,
            *[pltpu.VMEM((padded, n1), f32)] * 2,
            *[pltpu.VMEM((padded, n2), f32)] * 2,
            *[pltpu.VMEM((2, padded, LANES), f32)] * 8,
            pltpu.VMEM((slots, 2 * LANES), jnp.int32),
            pltpu.VMEM((slots, 2 * LANES), f32),
            pltpu.VMEM((slots, LANES), jnp.int32),
            pltpu.VMEM((slots, LANES), f32),
            pltpu.VMEM((slots, LANES), jnp.int32),
            pltpu.VMEM((slots, LANES), f32),
            pltpu.VMEM((2, slots, LANES), jnp.int32),
            pltpu.VMEM((2, slots, LANES), f32),
            pltpu.VMEM((2, slots, LANES), jnp.int32),
            pltpu.VMEM((2, slots, LANES), f32),
            pltpu.VMEM((2, padded, LANES), f32),
            pltpu.VMEM((padded, LANES), f32),
            pltpu.VMEM((2, padded, LANES), f32),
            pltpu.VMEM((padded, LANES), f32),
            pltpu.VMEM((padded, LANES), f32),
            pltpu.VMEM((n_lev, padded, LANES), f32),
            pltpu.SemaphoreType.DMA((14,)),
            pltpu.SemaphoreType.DMA((5, 2)),
            pltpu.SemaphoreType.DMA((5, 2)),
            pltpu.SemaphoreType.DMA((4, 2)),
            pltpu.SemaphoreType.DMA((4, 2)),
            pltpu.SemaphoreType.DMA((n_lev,)),
            pltpu.SemaphoreType.DMA((n_lev,)),
            pltpu.SemaphoreType.DMA((n2 // chunk,)),
            pltpu.SemaphoreType.DMA((n_lev,)),
        ],
        compiler_params=pltpu.CompilerParams(
            collective_id=0, has_side_effects=True, vmem_limit_bytes=16 << 20
        ),
    )(*(pltpu.with_memory_space_constraint(a, pltpu.HBM) for a in (jnp.transpose(field, (1, 0, 2)), *args[1:])))
    result = pl.pallas_call(
        transform,
        out_shape=jax.ShapeDtypeStruct((tracers, levels, chunk), f32),
        in_specs=[pl.BlockSpec(memory_space=pltpu.VMEM)] * 3,
        out_specs=pl.BlockSpec(memory_space=pltpu.VMEM),
        compiler_params=pltpu.CompilerParams(vmem_limit_bytes=8 << 20),
    )(gathered, jnp.asarray(t_high), jnp.asarray(t_low))
    return jnp.transpose(result, (1, 0, 2))


def solution(mesh):
    in_specs = (P("lev", None, "patch"),)
    in_specs += (P("patch", None, None),) * 4
    in_specs += (P(None, "patch"),) * 8
    out_specs = P(None, None, ("patch", "lev"))
    fn = functools.partial(on_device, mesh.shape["patch"], mesh.shape["lev"])
    return jax.shard_map(
        fn, mesh=mesh, in_specs=in_specs, out_specs=out_specs, check_vma=False
    )
```

time: 24.4 us -> 23.9 us (0.980)
  Pallas kernels: 24.3 us -> 23.7 us
    pallas_call x1, Pallas kernels: 22.9 us -> 22.4 us  [on_device(): pl.pallas_call(functools.partial(body, n_patch, n_lev, levels), out_shape...]
where the time goes in v3:
time: 23.9 us; the launch traced here: 23.8 us
  Pallas kernels  23.7 us (99%)
    pallas_call x1, Pallas kernels, on_device(): pl.pallas_call(functools.partial(body, n_patch, n_lev, levels), out_shape...  22.4 us
    pallas_call x1, Pallas kernels, on_device(): pl.pallas_call(transform, out_shape=jax.ShapeDtypeStruct((tracers, levels...  1.34 us

profile of v3, /device:TPU:0, one launch (start us, length us, event | category | flops | bytes accessed | tf_op | source)
XLA Modules:
  0.0 23.8 jit_solution(8982376033171358903)
XLA Ops:
  0.0 0.0 copy-start
  0.0 0.0 copy-start.1
  0.0 22.4 %shard_map.145.gathered = f32[4,64,512]{2,1,0:T(8,128)S(1)} custom-call(f32[3,20,2048]{2,1,0:T(8,128)} %bitcast.2, s32[1,2,128]{2,1,0:T(2,128)} %refs_1_.1, s32[1,2,128]{2,1,0:T(2,128)} %refs_2_.1, s32[1,2,64]{2,1,0:T(2,128)} %refs_3_.1, s32[1,2,64]{2,1,0:T(2,128)} %refs_4_.1, s32[8,1024]{1,0:T(8,128)} %refs_5_.1, f32[8,1024]{1,0:T(8,128)} %refs_6_.1, ...), custom_call_target="tpu_custom_call" | custom-call | tf_op jit(solution)/shard_map/pallas_call | solution.py:533
  22.4 0.0 copy-done
  22.4 0.0 copy-done.1
  22.4 1.3 %shard_map.146 = f32[3,80,512]{2,1,0:T(8,128)} custom-call(f32[4,64,512]{2,1,0:T(8,128)S(1)} %shard_map.145.gathered, bf16[240,256]{1,0:T(8,128)(2,1)S(1)} %copy-done.1, bf16[240,256]{1,0:T(8,128)(2,1)S(1)} %copy-done), custom_call_target="tpu_custom_call" | custom-call | tf_op jit(solution)/shard_map/pallas_call | solution.py:581
Async XLA Ops:
  0.0 22.4 %copy-start = (bf16[240,256]{1,0:T(8,128)(2,1)S(1)}, bf16[240,256]{1,0:T(8,128)(2,1)}, u32[]{:S(2)}) copy-start(bf16[240,256]{1,0:T(8,128)(2,1)} %constant.5.clone.t_low) | copy-start | bytes 368644
  0.0 22.4 %copy-start.1 = (bf16[240,256]{1,0:T(8,128)(2,1)S(1)}, bf16[240,256]{1,0:T(8,128)(2,1)}, u32[]{:S(2)}) copy-start(bf16[240,256]{1,0:T(8,128)(2,1)} %constant.4.clone.t_high) | copy-start | bytes 368644

commit v4 on v3

--- a/solution.py
+++ b/solution.py
@@ -62,6 +62,7 @@
         lane.append(link & (LANES - 1))
         block.append(link >> 7)
         weight.append(jnp.broadcast_to(weights[k : k + 1, cols], (SUB, LANES)))
+    room = merged.shape[0] // slots
     which = lax.broadcasted_iota(jnp.int32, (SUB, LANES), 0)
     same = [[lane[j] == lane[k] for j in range(k)] for k in range(slots)]
     for g in range(-(-blocks // SUB)):
@@ -72,9 +73,13 @@
             for j in range(k):
                 total = total + jnp.where(same[k][j], placed[j], 0.0)
             placed.append(mine)
-            merged[k, g * SUB : (g + 1) * SUB, :] = total
+            at = k * room + g * SUB
+            merged[at : at + SUB, :] = total
     none = jnp.zeros((2 * SUB - slots, LANES), jnp.float32)
-    tables = [halves(jnp.concatenate([merged[:, b, :], none], axis=0)) for b in range(blocks)]
+    tables = []
+    for b in range(blocks):
+        row = merged[pl.ds(b, slots, stride=room), :]
+        tables.append(halves(jnp.concatenate([row, none], axis=0)))
     short = [jnp.concatenate([v, v], axis=0).astype(jnp.int16) for v in lane]
     strips = []
     for s in range(LANES // (2 * SUB)):
@@ -124,7 +129,7 @@
             tail[1][:, cols] = spread(tiles, 1, own, blocks)
         return 0
 
-    lax.fori_loop(0, count // width, step, 0)
+    lax.fori_loop(0, count // width, step, 0, unroll=2 if count > width else 1)
 
 
 def prepare(links, weights, merged, count, blocks, out):
@@ -184,11 +189,11 @@
     given, gathered, held, rest = refs[:13], refs[13], refs[14:27], refs[27:]
     field, sc1, sd1, sc2, sd2, pl1, pw1, ul1, uw1, pl2, pw2, ul2, uw2 = held
     (
-        xs, ext, ext2, merged, t1h, t1l, t2h, t2l, w2h, w2l,
+        xs, ext, ext2, merged, t1h, t1l, w1h, w1l, w3h, w3l, w4h, w4l, p2h, p2l, w2h, w2l, qh, ql,
         det1, sm1, det2, sm2,
         asend, arecv, afar, bsend, brecv, csend, crecv, cfar,
-        link1, weight1, link2, weight2, link3, weight3, rlink1, rweight1, rlink2, rweight2,
-        fpart, own2, early1, early2, hsend, hrecv,
+        link1, weight1, link2, weight2, link3, weight3, link4, weight4, rlink1, rweight1, rlink2, rweight2,
+        fpart, own2, early1, hsend, hrecv,
         in_sem, x_send, x_recv, m_send, m_recv, g_send, g_recv, h_send, h_recv,
     ) = rest
     tracers, own, cells = field.shape
@@ -298,13 +303,6 @@
             def _():
                 gathered[d] = part[...]
 
-    def add_tail(into, n, tail, add):
-        for c in range(0, n, wide):
-            cols = slice(c, c + wide)
-            got = product(ext, padded, n1, *tail, cols)
-            old = into[:, cols]
-            into[:, cols] = old + got if add else old - got
-
     lower = lax.broadcasted_iota(jnp.int32, (padded, LANES), 1) < halo2
     first = lax.broadcasted_iota(jnp.int32, (SUB, LANES), 1) < halo2
 
@@ -326,104 +324,137 @@
     pack(n1, cells)
     for side in range(2):
         picked(xs, n1, b1, sc1[0, 1 - side : 2 - side, :], asend.at[side])
-    pl.semaphore_wait(barrier, 4 + n_lev - 1)
-    for side in range(2):
-        near1[side].start()
-        far1[side].start()
-
-    loaded(2, 5, 6, 13)
     put(ext, padded, 0, xs[:, n1:cells])
+    loaded(2, 5, 6, 13, 3, 4, 7, 8, 9, 10, 11, 12)
     pack(0, n1)
+
+    def fine1(cols, got):
+        det1[:, cols] = xs[:, cols] - got
+
+    def detail():
+        stage(pl1, pw1, merged, 0, n1, b1, e1 // LANES, ext, (t1h, t1l), fine1)
+
+    def level2():
+        prepare(link2, weight2, merged, LANES, b2, (w4h, w4l))
+        prepare(pl2, pw2, merged, n2, e2 // LANES, (p2h, p2l))
+        prepare(ul2, uw2, merged, n2, e2 // LANES, (w2h, w2l))
+
     for side in range(2):
         index = sd1[0, 1 - side : 2 - side, :]
         picked(pl1, 0, b1, index, half(link1, side))
         picked(pw1, 0, b1, index, half(weight1, side))
-        picked(xs, 0, b1, index, fpart.at[side])
-
-    def sent1(cols, got):
-        for side in range(2):
-            bsend[side] = fpart[side] - got[:, side * LANES : (side + 1) * LANES]
-
-    stage(link1, weight1, merged, 0, 2 * LANES, b1, b1, ext, None, sent1)
-    for copy in part1 + meta1:
-        copy.start()
-
-    def fine1(cols, got):
-        det1[:, cols] = xs[:, cols] - got
-
-    tail1 = (t1h, t1l)
-    stage(pl1, pw1, merged, 0, n1, b1, e1 // LANES, ext, tail1, fine1)
-
-    loaded(3, 4, 7, 8, 9, 10, 11, 12)
     picked(pl2, 0, b2, two(sd2), link2)
     picked(pw2, 0, b2, two(sd2), weight2)
-    for copy in meta2:
+    picked(ul1, 0, b2, two(sd2), link4)
+    picked(uw1, 0, b2, two(sd2), weight4)
+
+    @pl.when(patch < 2)
+    def _():
+        detail()
+        level2()
+
+    pl.semaphore_wait(barrier, 4 + n_lev - 1)
+    for copy in near1 + far1 + meta1 + meta2:
         copy.start()
+
+    @pl.when(patch >= 2)
+    def _():
+        detail()
+
+    for side in range(2):
+        picked(det1, 0, b1, sd1[0, 1 - side : 2 - side, :], bsend.at[side])
+    for copy in part1:
+        copy.start()
+    picked(xs, n1, b2, two(sd2), fpart.at[0])
+    prepare(ul1, uw1, merged, n1, e1 // LANES, (w1h, w1l))
+    prepare(link4, weight4, merged, LANES, e1 // LANES, (w3h, w3l))
+
+    @pl.when(patch >= 2)
+    def _():
+        level2()
 
     for side in range(2):
         near1[side].wait_recv()
         put(ext, padded, n1 + side * halo1, arecv[side])
-    add_tail(det1, n1, tail1, False)
+    for c in range(0, n1, wide):
+        cols = slice(c, c + wide)
+        det1[:, cols] = det1[:, cols] - product(ext, padded, n1, t1h, t1l, cols)
     scatter(det1, 0)
     put(ext, padded, 0, det1[...])
-
-    def coarse1(cols, got):
-        at = pl.ds(pl.multiple_of(cols.start + n1, LANES), cols.size)
-        sm1[:, cols] = xs[:, at] + got
-
-    stage(ul1, uw1, merged, 0, n1, b1, e1 // LANES, ext, tail1, coarse1)
-    for copy in meta1:
+    for copy in meta1 + far1:
         copy.wait_recv()
     for side in range(2):
-        early1[side] = reach(asend[1 - side], rlink1.at[side], rweight1.at[side], side1(1 - side))
+        known = reach(asend[1 - side], rlink1.at[side], rweight1.at[side], side1(1 - side))
+        outer = reach(afar[side], rlink1.at[side], rweight1.at[side], side1(side))
+        early1[side] = known + outer
     for side in range(2):
-        far1[side].wait_recv()
         part1[side].wait_recv()
-        value = brecv[side] - early1[side]
-        value = value - reach(afar[side], rlink1.at[side], rweight1.at[side], side1(side))
-        put(ext, padded, n1 + side * halo1, value)
-    add_tail(sm1, n1, tail1, True)
-
+        put(ext, padded, n1 + side * halo1, brecv[side] - early1[side])
+
+    def smooth(start, stop):
+        for c in range(start, stop, wide):
+            cols = slice(c, c + wide)
+            sm1[:, cols] = xs[:, n1 + c : n1 + c + wide] + product(ext, padded, 0, w1h, w1l, cols)
+
+    smooth(n2, n1)
     put(ext2, padded, 0, sm1[:, n2:n1])
     picked(sm1, n2, b2, two(sc2), own2)
-    picked(sm1, 0, b2, two(sd2), fpart.at[0])
-
-    def sent2(cols, got):
-        part = pltpu.roll(fpart[0] - got, halo2, axis=1)
-        csend[0] = jnp.where(lower, own2[...], part)
-        csend[1] = jnp.where(lower, part, own2[...])
-
-    stage(link2, weight2, merged, 0, LANES, b2, b2, ext2, None, sent2)
-    for side in range(2):
-        near2[side].start()
-        far2[side].start()
-
-    def fine2(cols, got):
+    every_lane = slice(0, LANES)
+    part = fpart[0] + product(ext, padded, 0, w3h, w3l, every_lane)
+    part = part - product(ext2, padded, 0, w4h, w4l, every_lane)
+    part = pltpu.roll(part, halo2, axis=1)
+    csend[0] = jnp.where(lower, own2[...], part)
+    csend[1] = jnp.where(lower, part, own2[...])
+    for copy in near2 + far2:
+        copy.start()
+
+    smooth(0, n2)
+    own_rows = slice(0, n2)
+    for c in range(0, n2, wide):
+        cols = slice(c, c + wide)
+        got = product(ext2, padded, 0, p2h.at[own_rows], p2l.at[own_rows], cols)
         det2[:, cols] = sm1[:, cols] - got
-
-    tail2 = (t2h, t2l)
-    stage(pl2, pw2, merged, 0, n2, b2, e2 // LANES, ext2, tail2, fine2)
     scatter(det2, n1)
-
-    prepare(ul2, uw2, merged, n2, e2 // LANES, (w2h, w2l))
+    put(ext2, padded, 0, det2[...])
     for copy in meta2:
         copy.wait_recv()
     turned = lax.broadcasted_iota(jnp.int32, (rlink2.shape[1], LANES), 1) < halo2
     link3[...] = jnp.where(turned, rlink2[0], rlink2[1])
     weight3[...] = jnp.where(turned, rweight2[0], rweight2[1])
-    early2[...] = reach(own2[...], link3, weight3, side2(False))
-
-    for side in range(2):
-        near2[side].wait_recv()
-    edge = jnp.where(lower, crecv[0], crecv[1])
-    hsend[...] = edge
+    put(ext2, padded, n2, -reach(own2[...], link3, weight3, side2(False)))
+
+    for c in range(0, n2, wide):
+        cols = slice(c, c + wide)
+        sm2[:, cols] = sm1[:, n2 + c : n2 + c + wide] + product(ext2, padded, 0, w2h, w2l, cols)
+    scatter(sm2, n1 + n2)
+
+    @pl.when(me >= (n1 + n2) // chunk)
+    def _():
+        for c in range(0, n2, wide):
+            cols = slice(c, c + wide)
+            both = jnp.concatenate([p2h[n2:e2, :], p2l[n2:e2, :]], axis=0)
+            both = jnp.dot(both, w2h[own_rows, cols], preferred_element_type=jnp.float32)
+            rest = jnp.dot(p2h[n2:e2, :], w2l[own_rows, cols], preferred_element_type=jnp.float32)
+            high, low = halves(-(both[0:LANES] + both[LANES : 2 * LANES] + rest))
+            qh[0:LANES, cols] = high
+            ql[0:LANES, cols] = low
+            qh[LANES : 2 * LANES, cols] = w2h[n2:e2, cols]
+            ql[LANES : 2 * LANES, cols] = w2l[n2:e2, cols]
+
+    for copy in near2 + far2:
+        copy.wait_recv()
+    hsend[0] = jnp.where(lower, crecv[0], crecv[1])
+    value = pltpu.roll(jnp.where(lower, crecv[1], crecv[0]), halo2, axis=1)
+    outer = jnp.where(lower, cfar[0], cfar[1])
+    hsend[1] = value - reach(outer, link3, weight3, side2(True))
 
     forward = []
-    for piece in range(n2 // chunk):
+    for piece in range(2 * n2 // chunk):
         d = n1 // chunk + piece
+        count = 1 if piece < n2 // chunk else 2
         copy = pltpu.make_async_remote_copy(
-            src_ref=hsend,
-            dst_ref=hrecv.at[me],
+            src_ref=hsend.at[0:count],
+            dst_ref=hrecv.at[me, 0:count],
             send_sem=h_send.at[piece],
             recv_sem=h_recv.at[me],
             device_id={"lev": d},
@@ -437,23 +468,7 @@
 
         @pl.when(me == d)
         def _():
-            hrecv[d] = edge
-
-    put(ext2, padded, n2, edge)
-    for c in range(0, n2, wide):
-        cols = slice(c, c + wide)
-        value = det2[:, cols] - product(ext2, padded, n2, *tail2, cols)
-        put(ext2, padded, c, value)
-
-    for side in range(2):
-        far2[side].wait_recv()
-    value = pltpu.roll(jnp.where(lower, crecv[1], crecv[0]), halo2, axis=1) - early2[...]
-    outer = jnp.where(lower, cfar[0], cfar[1])
-    put(ext2, padded, n2, value - reach(outer, link3, weight3, side2(True)))
-    for c in range(0, n2, wide):
-        cols = slice(c, c + wide)
-        sm2[:, cols] = sm1[:, n2 + c : n2 + c + wide] + product(ext2, padded, 0, w2h, w2l, cols)
-    scatter(sm2, n1 + n2)
+            hrecv[d, 0:count] = hsend[0:count]
 
     for s in range(n_lev):
 
@@ -468,31 +483,46 @@
                 device_id_type=MESH,
             ).wait_recv()
 
-    inner = (me >= n1 // chunk) & (me < (n1 + n2) // chunk)
-
-    @pl.when(inner)
-    def _():
+    def arrived(count):
         for s in range(n_lev):
 
             @pl.when(me != s)
             def _():
                 pltpu.make_async_remote_copy(
-                    src_ref=hrecv.at[s],
-                    dst_ref=hrecv.at[s],
+                    src_ref=hrecv.at[s, 0:count],
+                    dst_ref=hrecv.at[s, 0:count],
                     send_sem=h_send.at[0],
                     recv_sem=h_recv.at[s],
                     device_id={"lev": s},
                     device_id_type=MESH,
                 ).wait_recv()
 
-        at = pl.multiple_of((me - n1 // chunk) * chunk, LANES)
-        cols = pl.ds(at, chunk)
+    def times(value, high, low):
+        top, rest = halves(value)
+        count = value.shape[0]
+        both = jnp.concatenate([top, rest], axis=0)
+        both = jnp.dot(both, high, preferred_element_type=jnp.float32)
+        rest = jnp.dot(top, low, preferred_element_type=jnp.float32)
+        return both[0:count] + both[count : 2 * count] + rest
+
+    def every(which):
+        return jnp.concatenate([hrecv[s, which] for s in range(n_lev)], axis=0)
+
+    @pl.when((me >= n1 // chunk) & (me < (n1 + n2) // chunk))
+    def _():
+        arrived(1)
+        cols = pl.ds(pl.multiple_of((me - n1 // chunk) * chunk, LANES), chunk)
+        change = times(every(0), p2h[n2:e2, cols], p2l[n2:e2, cols])
         for s in range(n_lev):
-            high, low = halves(hrecv[s])
-            both = jnp.concatenate([high, low], axis=0)
-            both = jnp.dot(both, t2h[:, cols], preferred_element_type=jnp.float32)
-            rest = jnp.dot(high, t2l[:, cols], preferred_element_type=jnp.float32)
-            gathered[s] = gathered[s] - (both[0:padded] + both[padded : 2 * padded] + rest)
+            gathered[s] = gathered[s] - change[s * padded : (s + 1) * padded]
+
+    @pl.when(me >= (n1 + n2) // chunk)
+    def _():
+        arrived(2)
+        cols = pl.ds(pl.multiple_of((me - (n1 + n2) // chunk) * chunk, LANES), chunk)
+        change = times(jnp.concatenate([every(0), every(1)], axis=1), qh[:, cols], ql[:, cols])
+        for s in range(n_lev):
+            gathered[s] = gathered[s] + change[s * padded : (s + 1) * padded]
 
     for group in (near1, far1, part1, near2, far2, meta1, meta2):
         for copy in group:
@@ -541,15 +571,20 @@
             pltpu.VMEM((padded, cells), f32),
             pltpu.VMEM((2 * padded, e1), bf16),
             pltpu.VMEM((2 * padded, e2), bf16),
-            pltpu.VMEM((2, slots, -(-(e1 // LANES) // SUB) * SUB, LANES), f32),
+            pltpu.VMEM((2, slots * -(-(e1 // LANES) // SUB) * SUB, LANES), f32),
             *[pltpu.VMEM((e1 - n1, n1), bf16)] * 2,
-            *[pltpu.VMEM((e2 - n2, n2), bf16)] * 2,
-            *[pltpu.VMEM((e2, n2), bf16)] * 2,
+            *[pltpu.VMEM((e1, n1), bf16)] * 2,
+            *[pltpu.VMEM((e1, LANES), bf16)] * 2,
+            *[pltpu.VMEM((n2, LANES), bf16)] * 2,
+            *[pltpu.VMEM((e2, n2), bf16)] * 4,
+            *[pltpu.VMEM((2 * (e2 - n2), n2), bf16)] * 2,
             *[pltpu.VMEM((padded, n1), f32)] * 2,
             *[pltpu.VMEM((padded, n2), f32)] * 2,
             *[pltpu.VMEM((2, padded, LANES), f32)] * 8,
             pltpu.VMEM((slots, 2 * LANES), jnp.int32),
             pltpu.VMEM((slots, 2 * LANES), f32),
+            pltpu.VMEM((slots, LANES), jnp.int32),
+            pltpu.VMEM((slots, LANES), f32),
             pltpu.VMEM((slots, LANES), jnp.int32),
             pltpu.VMEM((slots, LANES), f32),
             pltpu.VMEM((slots, LANES), jnp.int32),
@@ -561,9 +596,8 @@
             pltpu.VMEM((2, padded, LANES), f32),
             pltpu.VMEM((padded, LANES), f32),
             pltpu.VMEM((2, padded, LANES), f32),
-            pltpu.VMEM((padded, LANES), f32),
-            pltpu.VMEM((padded, LANES), f32),
-            pltpu.VMEM((n_lev, padded, LANES), f32),
+            pltpu.VMEM((2, padded, LANES), f32),
+            pltpu.VMEM((n_lev, 2, padded, LANES), f32),
             pltpu.SemaphoreType.DMA((14,)),
             pltpu.SemaphoreType.DMA((5, 2)),
             pltpu.SemaphoreType.DMA((5, 2)),
@@ -571,11 +605,11 @@
             pltpu.SemaphoreType.DMA((4, 2)),
             pltpu.SemaphoreType.DMA((n_lev,)),
             pltpu.SemaphoreType.DMA((n_lev,)),
-            pltpu.SemaphoreType.DMA((n2 // chunk,)),
+            pltpu.SemaphoreType.DMA((2 * n2 // chunk,)),
             pltpu.SemaphoreType.DMA((n_lev,)),
         ],
         compiler_params=pltpu.CompilerParams(
-            collective_id=0, has_side_effects=True, vmem_limit_bytes=16 << 20
+            collective_id=0, has_side_effects=True, vmem_limit_bytes=24 << 20
         ),
     )(*(pltpu.with_memory_space_constraint(a, pltpu.HBM) for a in (jnp.transpose(field, (1, 0, 2)), *args[1:])))
     result = pl.pallas_call(

time: 23.9 us -> 22.7 us (0.950)
  Pallas kernels: 23.7 us -> 22.5 us
    pallas_call x1, Pallas kernels: 22.4 us -> 21.2 us  [on_device(): pl.pallas_call(functools.partial(body, n_patch, n_lev, levels), out_shape...]
where the time goes in v4:
time: 22.7 us; the launch traced here: 22.6 us
  Pallas kernels  22.5 us (99%)
    pallas_call x1, Pallas kernels, on_device(): pl.pallas_call(functools.partial(body, n_patch, n_lev, levels), out_shape...  21.2 us
    pallas_call x1, Pallas kernels, on_device(): pl.pallas_call(transform, out_shape=jax.ShapeDtypeStruct((tracers, levels...  1.34 us

profile of v4, /device:TPU:0, one launch (start us, length us, event | category | flops | bytes accessed | tf_op | source)
XLA Modules:
  0.0 22.6 jit_solution(6277206849517508981)
XLA Ops:
  0.0 0.0 copy-start
  0.0 0.0 copy-start.1
  0.0 21.2 %shard_map.145.gathered = f32[4,64,512]{2,1,0:T(8,128)S(1)} custom-call(f32[3,20,2048]{2,1,0:T(8,128)} %bitcast.2, s32[1,2,128]{2,1,0:T(2,128)} %refs_1_.1, s32[1,2,128]{2,1,0:T(2,128)} %refs_2_.1, s32[1,2,64]{2,1,0:T(2,128)} %refs_3_.1, s32[1,2,64]{2,1,0:T(2,128)} %refs_4_.1, s32[8,1024]{1,0:T(8,128)} %refs_5_.1, f32[8,1024]{1,0:T(8,128)} %refs_6_.1, ...), custom_call_target="tpu_custom_call" | custom-call | tf_op jit(solution)/shard_map/pallas_call | solution.py:563
  21.2 0.0 copy-done
  21.2 0.0 copy-done.1
  21.2 1.3 %shard_map.146 = f32[3,80,512]{2,1,0:T(8,128)} custom-call(f32[4,64,512]{2,1,0:T(8,128)S(1)} %shard_map.145.gathered, bf16[240,256]{1,0:T(8,128)(2,1)S(1)} %copy-done.1, bf16[240,256]{1,0:T(8,128)(2,1)S(1)} %copy-done), custom_call_target="tpu_custom_call" | custom-call | tf_op jit(solution)/shard_map/pallas_call | solution.py:615
Async XLA Ops:
  0.0 21.2 %copy-start = (bf16[240,256]{1,0:T(8,128)(2,1)S(1)}, bf16[240,256]{1,0:T(8,128)(2,1)}, u32[]{:S(2)}) copy-start(bf16[240,256]{1,0:T(8,128)(2,1)} %constant.5.clone.t_low) | copy-start | bytes 368644
  0.0 21.2 %copy-start.1 = (bf16[240,256]{1,0:T(8,128)(2,1)S(1)}, bf16[240,256]{1,0:T(8,128)(2,1)}, u32[]{:S(2)}) copy-start(bf16[240,256]{1,0:T(8,128)(2,1)} %constant.4.clone.t_high) | copy-start | bytes 368644

commit v5 on v4

--- a/solution.py
+++ b/solution.py
@@ -534,17 +534,22 @@
             copy.wait_send()
 
 
-def transform(gathered, t_high, t_low, out):
+def transform(gathered, t_high, t_low, out, staged, sems):
     groups, padded, chunk = gathered.shape
     tracers, levels, _ = out.shape
     high, low = halves(gathered[...].reshape(groups * padded, chunk))
+    copies = []
     for t in range(tracers):
         rows = slice(t * levels, (t + 1) * levels)
-        out[t] = (
+        staged[t] = (
             jnp.dot(t_high[rows, :], high, preferred_element_type=jnp.float32)
             + jnp.dot(t_high[rows, :], low, preferred_element_type=jnp.float32)
             + jnp.dot(t_low[rows, :], high, preferred_element_type=jnp.float32)
         )
+        copies.append(pltpu.make_async_copy(staged.at[t], out.at[t], sems.at[t]))
+        copies[t].start()
+    for copy in copies:
+        copy.wait()
 
 
 def on_device(n_patch, n_lev, *args):
@@ -616,7 +621,11 @@
         transform,
         out_shape=jax.ShapeDtypeStruct((tracers, levels, chunk), f32),
         in_specs=[pl.BlockSpec(memory_space=pltpu.VMEM)] * 3,
-        out_specs=pl.BlockSpec(memory_space=pltpu.VMEM),
+        out_specs=pl.BlockSpec(memory_space=pltpu.HBM),
+        scratch_shapes=[
+            pltpu.VMEM((tracers, levels, chunk), f32),
+            pltpu.SemaphoreType.DMA((tracers,)),
+        ],
         compiler_params=pltpu.CompilerParams(vmem_limit_bytes=8 << 20),
     )(gathered, jnp.asarray(t_high), jnp.asarray(t_low))
     return jnp.transpose(result, (1, 0, 2))

time: 22.7 us -> 22.6 us (level)
  no operation moved by 1% of the time
where the time goes in v5:
time: 22.6 us; the launch traced here: 22.5 us
  Pallas kernels  22.4 us (99%)
    pallas_call x1, Pallas kernels, on_device(): pl.pallas_call(functools.partial(body, n_patch, n_lev, levels), out_shape...  21.2 us
    pallas_call x1, Pallas kernels, on_device(): pl.pallas_call(transform, out_shape=jax.ShapeDtypeStruct((tracers, levels...  1.25 us

profile of v5, /device:TPU:0, one launch (start us, length us, event | category | flops | bytes accessed | tf_op | source)
XLA Modules:
  0.0 22.5 jit_solution(10269877602940832597)
XLA Ops:
  0.0 0.0 copy-start
  0.0 0.0 copy-start.1
  0.0 21.2 %shard_map.145.gathered = f32[4,64,512]{2,1,0:T(8,128)S(1)} custom-call(f32[3,20,2048]{2,1,0:T(8,128)} %bitcast.2, s32[1,2,128]{2,1,0:T(2,128)} %refs_1_.1, s32[1,2,128]{2,1,0:T(2,128)} %refs_2_.1, s32[1,2,64]{2,1,0:T(2,128)} %refs_3_.1, s32[1,2,64]{2,1,0:T(2,128)} %refs_4_.1, s32[8,1024]{1,0:T(8,128)} %refs_5_.1, f32[8,1024]{1,0:T(8,128)} %refs_6_.1, ...), custom_call_target="tpu_custom_call" | custom-call | tf_op jit(solution)/shard_map/pallas_call | solution.py:568
  21.2 0.0 copy-done
  21.2 0.0 copy-done.1
  21.2 1.3 %shard_map.146 = f32[3,80,512]{2,1,0:T(8,128)} custom-call(f32[4,64,512]{2,1,0:T(8,128)S(1)} %shard_map.145.gathered, bf16[240,256]{1,0:T(8,128)(2,1)S(1)} %copy-done.1, bf16[240,256]{1,0:T(8,128)(2,1)S(1)} %copy-done), custom_call_target="tpu_custom_call" | custom-call | tf_op jit(solution)/shard_map/pallas_call | solution.py:620
Async XLA Ops:
  0.0 21.2 %copy-start = (bf16[240,256]{1,0:T(8,128)(2,1)S(1)}, bf16[240,256]{1,0:T(8,128)(2,1)}, u32[]{:S(2)}) copy-start(bf16[240,256]{1,0:T(8,128)(2,1)} %constant.5.clone.t_low) | copy-start | bytes 368644
  0.0 21.2 %copy-start.1 = (bf16[240,256]{1,0:T(8,128)(2,1)S(1)}, bf16[240,256]{1,0:T(8,128)(2,1)}, u32[]{:S(2)}) copy-start(bf16[240,256]{1,0:T(8,128)(2,1)} %constant.4.clone.t_high) | copy-start | bytes 368644
